TPU v7x, 32 devices: a whole 2x2x4 slice. The times are simulated.
32 devices in a mesh: shard: 8 (over z, core), rep: 4 (over y, x).
Axes of the slice: x: 2, y: 2, z: 4, core: 2. Of those that a mesh axis runs over, the one named last changes fastest.
Arguments:
- tokens: bfloat16 [49152, 640], P(('shard', 'rep')), may hold values from -6 to 6
- seq_lengths: int32 [64], replicated, may hold values from 256 to 1024, as said below
- seq_device: int32 [64], replicated, may hold values from 0 to 31, as said below
- w_query: bfloat16 [640, 1024], P('shard'), may hold values from -0.25 to 0.25
- w_keyval: bfloat16 [640, 512], P('shard'), may hold values from -0.25 to 0.25
- w_project: bfloat16 [1024, 640], P('shard'), may hold values from -0.1875 to 0.1875
- w_gate: bfloat16 [640, 2048], P('shard'), may hold values from -0.25 to 0.25
- w_upward: bfloat16 [640, 2048], P('shard'), may hold values from -0.25 to 0.25
- w_down: bfloat16 [2048, 640], P('shard'), may hold values from -0.125 to 0.125
- gain_input: bfloat16 [640], P('shard'), may hold values from 0.5 to 2
- gain_query: bfloat16 [256], P('shard'), may hold values from 0.5 to 2
- gain_key: bfloat16 [256], P('shard'), may hold values from 0.5 to 2
- gain_attend: bfloat16 [640], P('shard'), may hold values from 0.5 to 2
- gain_before: bfloat16 [640], P('shard'), may hold values from 0.5 to 2
- gain_after: bfloat16 [640], P('shard'), may hold values from 0.5 to 2
- cotangent: bfloat16 [49152, 640], P(('shard', 'rep')), may hold values from -6 to 6
Outputs:
- activations: bfloat16 [49152, 640], P(('shard', 'rep'))
- input_grad: float32 [49152, 640], P(('shard', 'rep'))
- query_grad: float32 [640, 1024], P('shard')
- keyval_grad: float32 [640, 512], P('shard')
- project_grad: float32 [1024, 640], P('shard')
- gate_grad: float32 [640, 2048], P('shard')
- upward_grad: float32 [640, 2048], P('shard')
- down_grad: float32 [2048, 640], P('shard')
- inputgain_grad: float32 [640], P('shard')
- querygain_grad: float32 [256], P('shard')
- keygain_grad: float32 [256], P('shard')
- attendgain_grad: float32 [640], P('shard')
- beforegain_grad: float32 [640], P('shard')
- aftergain_grad: float32 [640], P('shard')
Inputs may be any that keep to these rules, and one draw needn't show every extreme that they name: `seq_lengths`: some sequence has exactly 1024 tokens. `seq_device`: every device index holds exactly two sequences, whose lengths sum to at most 1536; on some device they sum to exactly 1536.
All inputs are finite; a program needn't handle non-finite values.
Results may differ from a plain program's by a relative error of at most 0.017.
Values may be sent and summed in bfloat16 or wider, within the bound.
A program may use at most 256 MiB of HBM per device.

v0:
```python
import jax
import jax.numpy as jnp
from jax import lax
from jax.sharding import PartitionSpec as P

QH = 4
HD = 256


EPS = 1e-06
THETA = 1000000.0
NEG = -1e30


def normed(value, gain):
    return value * lax.rsqrt(jnp.mean(value * value, axis=-1, keepdims=True) + EPS) * gain


def rotary(position, width):
    freqs = THETA ** (-(jnp.arange(width // 2, dtype=jnp.float32) * 2.0 / width))
    angles = position.astype(jnp.float32)[:, None] * freqs[None, :]
    return (jnp.cos(angles), jnp.sin(angles))


def rotate(value, cosine, sine):
    half = value.shape[-1] // 2
    first = value[..., :half]
    second = value[..., half:]
    return jnp.concatenate(
        [first * cosine - second * sine, second * cosine + first * sine], axis=-1
    )


def layout(seq_lengths, seq_device, device, rows):
    mine = seq_device == device
    lens = jnp.where(mine, seq_lengths, 0)
    ends = jnp.cumsum(lens, dtype=jnp.int32)
    starts = ends - lens
    row_ids = jnp.arange(rows, dtype=jnp.int32)
    begun = mine[None, :] & (starts[None, :] <= row_ids[:, None])
    segment = jnp.sum(begun.astype(jnp.int32), axis=1, dtype=jnp.int32)
    own_start = jnp.max(jnp.where(begun, starts[None, :], 0), axis=1)
    position = row_ids - own_start
    live = row_ids < jnp.sum(lens, dtype=jnp.int32)
    return (segment, position, live)


def left_dot(left, right):
    return lax.dot_general(
        left, right, (((0,), (0,)), ((), ())), preferred_element_type=jnp.float32
    )


def right_dot(left, right):
    return lax.dot_general(
        left, right, (((1,), (1,)), ((), ())), preferred_element_type=jnp.float32
    )


def shards(
    tokens,
    seq_lengths,
    seq_device,
    w_query,
    w_keyval,
    w_project,
    w_gate,
    w_upward,
    w_down,
    gain_input,
    gain_query,
    gain_key,
    gain_attend,
    gain_before,
    gain_after,
    cotangent,
):
    rows = tokens.shape[0]
    device = lax.axis_index("shard") * lax.axis_size("rep") + lax.axis_index("rep")
    segment, position, live = layout(seq_lengths, seq_device, device, rows)
    cosine, sine = rotary(position, HD)
    attn_full = (
        lax.all_gather(w_query, "shard", axis=0, tiled=True),
        lax.all_gather(w_keyval, "shard", axis=0, tiled=True),
        lax.all_gather(w_project, "shard", axis=0, tiled=True),
        lax.all_gather(gain_input, "shard", axis=0, tiled=True),
        lax.all_gather(gain_query, "shard", axis=0, tiled=True),
        lax.all_gather(gain_key, "shard", axis=0, tiled=True),
        lax.all_gather(gain_attend, "shard", axis=0, tiled=True),
    )
    ffn_full = (
        lax.all_gather(w_gate, "shard", axis=0, tiled=True),
        lax.all_gather(w_upward, "shard", axis=0, tiled=True),
        lax.all_gather(w_down, "shard", axis=0, tiled=True),
        lax.all_gather(gain_before, "shard", axis=0, tiled=True),
        lax.all_gather(gain_after, "shard", axis=0, tiled=True),
    )
    query_full, keyval_full, project_full, input_full, qgain_full, kgain_full, attend_full = (
        attn_full
    )
    gate_full, upward_full, down_full, before_full, after_full = ffn_full
    x_rows = tokens.astype(jnp.float32)
    h_value, back_input = jax.vjp(normed, x_rows, input_full.astype(jnp.float32))
    h_low = h_value.astype(jnp.bfloat16)
    q_raw = jnp.dot(h_low, query_full, preferred_element_type=jnp.float32).reshape(rows, QH, HD)
    kv_raw = jnp.dot(h_low, keyval_full, preferred_element_type=jnp.float32)

    def query_side(value, gain):
        return rotate(normed(value, gain), cosine[:, None, :], sine[:, None, :])

    def key_side(value, gain):
        return rotate(normed(value, gain), cosine, sine)

    q_rot, back_query = jax.vjp(query_side, q_raw, qgain_full.astype(jnp.float32))
    k_rot, back_key = jax.vjp(key_side, kv_raw[:, :HD], kgain_full.astype(jnp.float32))
    q_low = q_rot.astype(jnp.bfloat16)
    k_low = k_rot.astype(jnp.bfloat16)
    v_low = kv_raw[:, HD:].astype(jnp.bfloat16)
    block = rows // 3
    scale = HD ** (-0.5)
    row_ids = jnp.arange(rows, dtype=jnp.int32)

    def block_scores(index):
        q_block = q_low[index * block : (index + 1) * block]
        raw = jnp.einsum("qhd,kd->hqk", q_block, k_low, preferred_element_type=jnp.float32) * scale
        seg_block = segment[index * block : (index + 1) * block]
        row_block = row_ids[index * block : (index + 1) * block]
        allowed = (seg_block[:, None] == segment[None, :]) & (
            row_ids[None, :] <= row_block[:, None]
        )
        return (jnp.where(allowed[None], raw, NEG), q_block)

    out_parts = []
    lse_parts = []
    for index in range(3):
        logits, q_block = block_scores(index)
        peak = jnp.max(logits, axis=-1, keepdims=True)
        expo = jnp.exp(logits - peak)
        total = jnp.sum(expo, axis=-1, keepdims=True)
        probs = expo / total
        out_parts.append(
            jnp.einsum(
                "hqk,kd->qhd", probs.astype(jnp.bfloat16), v_low, preferred_element_type=jnp.float32
            )
        )
        lse_parts.append(peak + jnp.log(total))
    attended = jnp.concatenate(out_parts, axis=0).reshape(rows, QH * HD).astype(jnp.bfloat16)
    branch = jnp.dot(attended, project_full, preferred_element_type=jnp.float32)
    branch_normed, back_attend = jax.vjp(normed, branch, attend_full.astype(jnp.float32))
    x_mid = x_rows + branch_normed
    h_two, back_before = jax.vjp(normed, x_mid, before_full.astype(jnp.float32))
    h_two_low = h_two.astype(jnp.bfloat16)
    gate = jnp.dot(h_two_low, gate_full, preferred_element_type=jnp.float32)
    upper = jnp.dot(h_two_low, upward_full, preferred_element_type=jnp.float32)
    hidden, back_glu = jax.vjp(
        lambda g_val, u_val: jax.nn.gelu(g_val, approximate=True) * u_val, gate, upper
    )
    hidden_low = hidden.astype(jnp.bfloat16)
    ffn = jnp.dot(hidden_low, down_full, preferred_element_type=jnp.float32)
    ffn_normed, back_after = jax.vjp(normed, ffn, after_full.astype(jnp.float32))
    activations = (x_mid + ffn_normed).astype(jnp.bfloat16)
    gate_back, upward_back, down_back = (
        lax.all_gather(w_gate, "shard", axis=0, tiled=True),
        lax.all_gather(w_upward, "shard", axis=0, tiled=True),
        lax.all_gather(w_down, "shard", axis=0, tiled=True),
    )
    query_back, keyval_back, project_back = (
        lax.all_gather(w_query, "shard", axis=0, tiled=True),
        lax.all_gather(w_keyval, "shard", axis=0, tiled=True),
        lax.all_gather(w_project, "shard", axis=0, tiled=True),
    )
    upstream = jnp.where(live[:, None], cotangent.astype(jnp.float32), jnp.float32(0.0))
    d_ffn, aftergain_grad = back_after(upstream)
    d_ffn_low = d_ffn.astype(jnp.bfloat16)
    down_grad = left_dot(hidden_low, d_ffn_low)
    d_hidden = right_dot(d_ffn_low, down_back)
    d_gate, d_up = back_glu(d_hidden)
    d_gate_low = d_gate.astype(jnp.bfloat16)
    d_up_low = d_up.astype(jnp.bfloat16)
    gate_grad = left_dot(h_two_low, d_gate_low)
    upward_grad = left_dot(h_two_low, d_up_low)
    d_h_two = right_dot(d_gate_low, gate_back) + right_dot(d_up_low, upward_back)
    d_mid_part, beforegain_grad = back_before(d_h_two)
    d_mid = upstream + d_mid_part
    d_branch, attendgain_grad = back_attend(d_mid)
    d_branch_low = d_branch.astype(jnp.bfloat16)
    project_grad = left_dot(attended, d_branch_low)
    d_attended = right_dot(d_branch_low, project_back).reshape(rows, QH, HD).astype(jnp.bfloat16)
    dq_parts = []
    d_keys = jnp.zeros((rows, HD), jnp.float32)
    d_values = jnp.zeros((rows, HD), jnp.float32)
    for index in range(3):
        logits, q_block = block_scores(index)
        probs = jnp.exp(logits - lse_parts[index])
        d_block = d_attended[index * block : (index + 1) * block]
        d_probs = jnp.einsum("qhd,kd->hqk", d_block, v_low, preferred_element_type=jnp.float32)
        spread = jnp.sum(probs * d_probs, axis=-1, keepdims=True)
        d_logits = (probs * (d_probs - spread)).astype(jnp.bfloat16)
        dq_parts.append(
            jnp.einsum("hqk,kd->qhd", d_logits, k_low, preferred_element_type=jnp.float32) * scale
        )
        d_keys = (
            d_keys
            + jnp.einsum("hqk,qhd->kd", d_logits, q_block, preferred_element_type=jnp.float32)
            * scale
        )
        d_values = d_values + jnp.einsum(
            "hqk,qhd->kd", probs.astype(jnp.bfloat16), d_block, preferred_element_type=jnp.float32
        )
    d_queries = jnp.concatenate(dq_parts, axis=0)
    d_q_raw, querygain_grad = back_query(d_queries)
    d_k_raw, keygain_grad = back_key(d_keys)
    d_q_low = d_q_raw.reshape(rows, QH * HD).astype(jnp.bfloat16)
    d_kv_low = jnp.concatenate([d_k_raw, d_values], axis=1).astype(jnp.bfloat16)
    query_grad = left_dot(h_low, d_q_low)
    keyval_grad = left_dot(h_low, d_kv_low)
    d_h = right_dot(d_q_low, query_back) + right_dot(d_kv_low, keyval_back)
    d_input_part, inputgain_grad = back_input(d_h)
    input_grad = d_mid + d_input_part
    all_shares = (
        lax.psum_scatter(query_grad, "shard", scatter_dimension=0, tiled=True),
        lax.psum_scatter(keyval_grad, "shard", scatter_dimension=0, tiled=True),
        lax.psum_scatter(project_grad, "shard", scatter_dimension=0, tiled=True),
        lax.psum_scatter(gate_grad, "shard", scatter_dimension=0, tiled=True),
        lax.psum_scatter(upward_grad, "shard", scatter_dimension=0, tiled=True),
        lax.psum_scatter(down_grad, "shard", scatter_dimension=0, tiled=True),
        lax.psum_scatter(inputgain_grad, "shard", scatter_dimension=0, tiled=True),
        lax.psum_scatter(querygain_grad, "shard", scatter_dimension=0, tiled=True),
        lax.psum_scatter(keygain_grad, "shard", scatter_dimension=0, tiled=True),
        lax.psum_scatter(attendgain_grad, "shard", scatter_dimension=0, tiled=True),
        lax.psum_scatter(beforegain_grad, "shard", scatter_dimension=0, tiled=True),
        lax.psum_scatter(aftergain_grad, "shard", scatter_dimension=0, tiled=True),
    )
    all_sums = lax.psum(
        (
            all_shares[0],
            all_shares[1],
            all_shares[2],
            all_shares[3],
            all_shares[4],
            all_shares[5],
            all_shares[6],
            all_shares[7],
            all_shares[8],
            all_shares[9],
            all_shares[10],
            all_shares[11],
        ),
        "rep",
    )
    (
        sum_query,
        sum_keyval,
        sum_project,
        sum_gate,
        sum_upward,
        sum_down,
        sum_input,
        sum_qgain,
        sum_kgain,
        sum_attend,
        sum_before,
        sum_after,
    ) = all_sums
    return (
        activations,
        input_grad,
        sum_query,
        sum_keyval,
        sum_project,
        sum_gate,
        sum_upward,
        sum_down,
        sum_input,
        sum_qgain,
        sum_kgain,
        sum_attend,
        sum_before,
        sum_after,
    )


def solution(mesh):
    return jax.shard_map(
        shards,
        mesh=mesh,
        in_specs=(
            P(("shard", "rep"), None),
            P(),
            P(),
            P("shard", None),
            P("shard", None),
            P("shard", None),
            P("shard", None),
            P("shard", None),
            P("shard", None),
            P("shard"),
            P("shard"),
            P("shard"),
            P("shard"),
            P("shard"),
            P("shard"),
            P(("shard", "rep"), None),
        ),
        out_specs=(
            P(("shard", "rep"), None),
            P(("shard", "rep"), None),
            P("shard", None),
            P("shard", None),
            P("shard", None),
            P("shard", None),
            P("shard", None),
            P("shard", None),
            P("shard"),
            P("shard"),
            P("shard"),
            P("shard"),
            P("shard"),
            P("shard"),
        ),
        check_vma=False,
    )
```

profile of v0, /device:TPU:0, one launch (start us, length us, event | category | flops | bytes accessed | tf_op | source)
XLA Modules:
  0.0 722.9 jit_solution(8640977445220974161)
XLA Ops:
  22.6 18.7 %all-reduce.19 = (bf16[640]{0:T(1024)(128)(2,1)S(1)}, bf16[256]{0:T(256)(128)(2,1)S(1)}, bf16[256]{0:T(256)(128)(2,1)S(1)}, bf16[640]{0:T(1024)(128)(2,1)S(1)}, ...) all-reduce(bf16[640]{0:T(1024)(128)(2,1)S(1)} %dynamic-update-slice, ...), channel_id=1, replica_groups=mesh['shard'=8,'rep'=4] {'shard'}, use_global_device_ids=true, to_apply=%add.4 | all-reduce | flops 3072 | bytes 12288
  44.3 18.5 %all_gather.43 = bf16[640,512]{1,0:T(8,128)(2,1)} all-gather(bf16[80,512]{1,0:T(8,128)(2,1)} %param.20), channel_id=1, replica_groups=mesh['shard'=8,'rep'=4] {'shard'}, dimensions={0}, use_global_device_ids=true | all-gather | bytes 737280 | tf_op jit(solution)/shard_map/all_gather | solution.py:84
  62.8 2.7 copy.155
  66.8 4.0 copy.166
  70.8 3.2 fusion.116
  75.2 4.1 fusion.89
  84.0 3.9 fusion.46
  87.9 8.0 %multiply_reduce_fusion.2 = (f32[1536,4]{0,1:T(4,128)}, f32[1536,1024]{0,1:T(8,128)}) fusion(bf16[640,1024]{1,0:T(8,128)(2,1)} %all-gather.6.cloned.1.call-done, bf16[1536,640]{0,1:T(8,128)(2,1)} %copy-done.12, f32[640]{0:T(1024)} %copy-done.66, f32[1536]{0:T(1024)S(1)} %copy-done.63), kind=kOutput, calls=%fused_computation.62 | convolution fusion | flops 2020337664 | bytes 9601536 | tf_op jit(solution)/shard_map/dot_general | solution.py:105
  96.0 6.6 copy.157
  103.9 3.7 multiply_multiply_fusion.3
  109.0 2.7 fusion.122
  113.5 2.8 copy-done.1
  116.3 3.4 fusion.76
  119.7 2.6 fusion.124
  124.1 2.9 copy-done
  127.1 3.8 fusion.74
  131.0 2.6 fusion.123
  135.4 2.9 copy-done.2
  138.3 2.7 fusion.75
  141.4 4.8 multiply_reduce_fusion.11
  150.5 10.4 %fusion.131 = f32[1536,2048]{1,0:T(8,128)} fusion(bf16[1536,640]{0,1:T(8,128)(2,1)S(1)} %multiply_convert_fusion.2, bf16[640,2048]{1,0:T(8,128)(2,1)} %all-gather.10.cloned.1.call-done), kind=kOutput, calls=%fused_computation.211 | convolution fusion | flops 4026531840 | bytes 17170432 | tf_op jit(solution)/shard_map/dot_general | solution.py:153
  160.9 16.8 %multiply_convert_fusion.1 = (bf16[1536,2048]{1,0:T(8,128)(2,1)}, f32[1536,2048]{1,0:T(8,128)}) fusion(f32[1536,2048]{1,0:T(8,128)} %fusion.131, bf16[1536,640]{0,1:T(8,128)(2,1)S(1)} %multiply_convert_fusion.2, bf16[640,2048]{1,0:T(8,128)(2,1)} %all-gather.12.cloned.1.call-done), kind=kOutput, calls=%fused_computation.31 | convolution fusion | flops 4057989120 | bytes 36044800 | tf_op jit(solution)/shard_map/dot_general | solution.py:154
  177.7 7.5 %multiply_reduce_fusion.9 = (f32[1536]{0:T(1024)S(1)}, f32[1536,640]{0,1:T(8,128)S(1)}) fusion(bf16[1536,2048]{1,0:T(8,128)(2,1)} %get-tuple-element.148, bf16[2048,640]{1,0:T(8,128)(2,1)} %all-gather.14.cloned.1.call-done), kind=kOutput, calls=%fused_computation.90 | convolution fusion | flops 4028496384 | bytes 12851200 | tf_op jit(solution)/shard_map/dot_general | solution.py:159
  187.3 3.1 fusion.39
  190.4 24.2 %multiply_convert_fusion = (bf16[1536,2048]{1,0:T(8,128)(2,1)}, bf16[1536,2048]{1,0:T(8,128)(2,1)}) fusion(f32[1536,2048]{1,0:T(8,128)} %fusion.131, f32[1536,2048]{1,0:T(8,128)} %get-tuple-element.149, bf16[1536,640]{0,1:T(8,128)(2,1)} %get-tuple-element.119, bf16[2048,640]{1,0:T(8,128)(2,1)} %all-gather.14.cloned.1.call-done), kind=kOutput, calls=%fused_computation.30 | convolution fusion | flops 4102029312 | bytes 42336256 | tf_op jit(solution)/shard_map/dot_general | solution.py:55
  214.6 7.8 %fusion.132 = f32[1536,640]{0,1:T(8,128)S(1)} fusion(bf16[1536,2048]{1,0:T(8,128)(2,1)} %get-tuple-element.114, bf16[640,2048]{1,0:T(8,128)(2,1)} %all-gather.10.cloned.1.call-done), kind=kOutput, calls=%fused_computation.212 | convolution fusion | flops 4026531840 | bytes 12845056 | tf_op jit(solution)/shard_map/dot_general | solution.py:55
  222.4 5.5 multiply_reduce_fusion.4
  227.9 3.1 multiply_reduce_fusion.5
  233.4 2.8 convolution_convert_fusion
  238.2 3.0 fusion.49
  241.2 5.8 fusion.13
  247.0 10.5 %fusion.10 = (f32[4,512]{1,0:T(4,128)S(1)}, f32[1536,512,4]{1,0,2:T(8,128)}) fusion(f32[4,512,1536]{1,2,0:T(8,128)} %copy-done.2, f32[4,512]{1,0:T(4,128)S(1)} %log_add_fusion.1, bf16[512,4,256]{0,2,1:T(8,128)(2,1)S(1)} %bitcast.163, f32[1536,512]{0,1:T(8,128)S(1)} %copy-done.6), kind=kOutput, calls=%fused_computation.16 | convolution fusion | flops 1620047872 | bytes 27017216 | tf_op jit(solution)/shard_map/qhd,kd->hqk/dot_general | solution.py:196
  257.5 8.2 %fusion.61 = f32[1536,256]{0,1:T(8,128)} fusion(f32[1536,256]{0,1:T(8,128)} %fusion.49, bf16[512,4,256]{0,2,1:T(8,128)(2,1)S(1)} %bitcast.164, f32[4,512,1536]{1,2,0:T(8,128)} %copy-done.2, f32[4,512]{1,0:T(4,128)S(1)} %log_add_fusion.1), kind=kOutput, calls=%fused_computation.119 | convolution fusion | flops 1617297408 | bytes 16785408 | tf_op jit(solution)/shard_map/hqk,qhd->kd/dot_general | solution.py:207
  265.7 7.1 fusion.7
  272.9 4.2 fusion.67
  277.1 9.7 %fusion.9 = bf16[4,512,1536]{1,2,0:T(8,128)(2,1)} fusion(f32[1536,512,4]{1,0,2:T(8,128)} %get-tuple-element.154, f32[4,512,1536]{1,2,0:T(8,128)S(1)} %bitcast.154, f32[4,512]{1,0:T(4,128)S(1)} %get-tuple-element.153, f32[4,512]{1,0:T(4,128)S(1)} %log_add_fusion), kind=kLoop, calls=%fused_computation.13 | loop fusion | flops 12582912 | bytes 31473664 | tf_op jit(solution)/shard_map/convert_element_type | solution.py:198
  286.8 5.8 convolution_bitcast_fusion
  292.6 13.3 %fusion.12 = bf16[4,512,1536]{1,2,0:T(8,128)(2,1)} fusion(f32[1536,512,4]{1,0,2:T(8,128)} %get-tuple-element.156, f32[4,512,1536]{1,2,0:T(8,128)} %copy-done.2, f32[4,512]{1,0:T(4,128)S(1)} %get-tuple-element.155, f32[4,512]{1,0:T(4,128)S(1)} %log_add_fusion.1), kind=kLoop, calls=%fused_computation.18 | loop fusion | flops 12582912 | bytes 31473664 | tf_op jit(solution)/shard_map/convert_element_type | solution.py:198
  305.9 5.8 convolution_bitcast_fusion.1
  311.7 5.4 fusion.15
  317.2 5.5 fusion.66
  322.8 3.1 fusion.92
  330.0 6.7 fusion.133
  337.2 5.6 multiply_bitcast_fusion
  342.8 5.6 multiply_bitcast_fusion.1
  348.5 3.9 multiply_bitcast_fusion.2
  357.0 2.5 multiply_reduce_fusion
  359.6 3.8 fusion.22
  363.4 4.6 copy.183
  368.0 5.7 fusion.112
  373.8 9.4 %fusion.136 = f32[2048,640]{1,0:T(8,128)} fusion(bf16[1536,2048]{1,0:T(8,128)(2,1)} %get-tuple-element.148, bf16[1536,640]{0,1:T(8,128)(2,1)} %get-tuple-element.119), kind=kOutput, calls=%fused_computation.216 | convolution fusion | flops 4026531840 | bytes 13500416 | tf_op jit(solution)/shard_map/dot_general | solution.py:49
  383.3 10.1 %fusion.134 = f32[640,2048]{1,0:T(8,128)} fusion(bf16[1536,640]{0,1:T(8,128)(2,1)} %copy-done.26, bf16[1536,2048]{1,0:T(8,128)(2,1)} %get-tuple-element.114), kind=kOutput, calls=%fused_computation.214 | convolution fusion | flops 4026531840 | bytes 13500416 | tf_op jit(solution)/shard_map/dot_general | solution.py:49
  393.5 10.1 %fusion.135 = f32[640,2048]{1,0:T(8,128)} fusion(bf16[1536,640]{0,1:T(8,128)(2,1)} %copy-done.26, bf16[1536,2048]{1,0:T(8,128)(2,1)} %get-tuple-element.113), kind=kOutput, calls=%fused_computation.215 | convolution fusion | flops 4026531840 | bytes 13500416 | tf_op jit(solution)/shard_map/dot_general | solution.py:49
  403.7 35.3 %reduce-scatter.7.cloned.1.call-done = f32[80,1024]{1,0:T(8,128)} async-done(((f32[640,1024]{1,0:T(8,128)}), f32[80,1024]{1,0:T(8,128)}) %reduce-scatter.7.cloned.1.call-update) | async-done | bytes 327696 | tf_op jit(solution)/shard_map/reduce_scatter | solution.py:221
  439.0 61.4 %reduce-scatter.17.cloned.1.call-done = f32[256,640]{1,0:T(8,128)} async-done(((f32[2048,640]{1,0:T(8,128)}), f32[256,640]{1,0:T(8,128)}) %reduce-scatter.17.cloned.1.call-update) | async-done | bytes 655376 | tf_op jit(solution)/shard_map/reduce_scatter | solution.py:226
  500.3 60.4 %reduce-scatter.13.cloned.1.call-done = f32[80,2048]{1,0:T(8,128)} async-done(((f32[640,2048]{1,0:T(8,128)}), f32[80,2048]{1,0:T(8,128)}) %reduce-scatter.13.cloned.1.call-update) | async-done | bytes 655376 | tf_op jit(solution)/shard_map/reduce_scatter | solution.py:224
  560.8 60.6 %reduce-scatter.15.cloned.1.call-done = f32[80,2048]{1,0:T(8,128)} async-done(((f32[640,2048]{1,0:T(8,128)}), f32[80,2048]{1,0:T(8,128)}) %reduce-scatter.15.cloned.1.call-update) | async-done | bytes 655376 | tf_op jit(solution)/shard_map/reduce_scatter | solution.py:225
  622.7 4.2 copy.195
  626.9 4.9 fusion.137
  633.9 3.2 fusion.42
  637.2 5.5 copy.196
  642.7 26.3 %all-reduce.16 = (f32[640]{0:T(1024)S(1)}, f32[256]{0:T(256)S(1)}, f32[256]{0:T(256)S(1)}, f32[640]{0:T(1024)S(1)}, f32[640]{0:T(1024)S(1)}, /*index=5*/f32[640]{0:T(1024)S(1)}) all-reduce(f32[640]{0:T(1024)S(1)} %get-tuple-element.78, f32[256]{0:T(256)S(1)} %get-tuple-element.70, ...), channel_id=8, replica_groups=mesh['shard'=8,'rep'=4] {'shard'}, use_global_device_ids=true, to_apply=%region_38.39.clone | all-reduce | flops 3072 | bytes 24576
  669.4 10.8 %all-reduce.17 = (f32[80]{0:T(128)}, f32[32]{0:T(128)}, f32[32]{0:T(128)}, f32[80]{0:T(128)}, f32[80]{0:T(128)}, /*index=5*/f32[80]{0:T(128)}) all-reduce(f32[80]{0:T(128)S(1)} %dynamic-slice.7, f32[32]{0:T(128)S(1)} %dynamic-slice.9, f32[32]{0:T(128)S(1)} %dynamic-slice.11, ...), channel_id=1, replica_groups=mesh['shard'=8,'rep'=4] {'rep'}, use_global_device_ids=true, to_apply=%region_39.40 | all-reduce | flops 384 | bytes 3072 | tf_op jit(solution)/shard_map/psum | solution.py:234
  680.2 25.8 %all-reduce.22.cloned.1.call-done = (f32[80,1024]{1,0:T(8,128)}, f32[80,512]{1,0:T(8,128)}, f32[128,640]{1,0:T(8,128)}, f32[80,2048]{1,0:T(8,128)}, f32[80,2048]{1,0:T(8,128)}, /*index=5*/f32[256,640]{1,0:T(8,128)}) async-done(((f32[80,1024]{1,0:T(8,128)}, f32[80,512]{1,0:T(8,128)}, f32[128,640]{1,0:T(8,128)}, f32[80,2048]{1,0:T(8,128)}, f32[80,2048]{1,0:T(8,128)}, /*index=5*/f32[256,640]{1,0:T(8,128)}), ...) | async-done | bytes 2785296 | tf_op jit(solution)/shard_map/psum | solution.py:234
  (302 shorter events, 64.7 us)
Async XLA Ops:
  7.2 80.7 %all-gather.6.cloned.1.call-start = ((), (), s32[]{:S(2)}) async-start(), calls=%async_computation.6 | async-start | bytes 1474560 | tf_op jit(solution)/shard_map/all_gather | solution.py:83
  7.9 133.4 %all-gather.8.cloned.1.call-start = ((), (), s32[]{:S(2)}) async-start(), calls=%async_computation.7 | async-start | bytes 1474560 | tf_op jit(solution)/shard_map/all_gather | solution.py:85
  8.7 141.8 %all-gather.10.cloned.1.call-start = ((), (), s32[]{:S(2)}) async-start(), calls=%async_computation.8 | async-start | bytes 2949120 | tf_op jit(solution)/shard_map/all_gather | solution.py:92
  9.4 151.5 %all-gather.12.cloned.1.call-start = ((), (), s32[]{:S(2)}) async-start(), calls=%async_computation.9 | async-start | bytes 2949120 | tf_op jit(solution)/shard_map/all_gather | solution.py:93
  10.0 167.7 %all-gather.14.cloned.1.call-start = ((), (), s32[]{:S(2)}) async-start(), calls=%async_computation.10 | async-start | bytes 2949120 | tf_op jit(solution)/shard_map/all_gather | solution.py:94
  10.6 393.1 %reduce-scatter.9.cloned.1.call-start = ((), (), s32[]{:S(2)}) async-start(), calls=%async_computation.12 | async-start | bytes 1474560 | tf_op jit(solution)/shard_map/reduce_scatter | solution.py:222
  41.9 32.3 %copy-start.70 = (f32[256]{0:T(256)}, f32[256]{0:T(256)S(1)}, u32[]{:S(2)}) copy-start(f32[256]{0:T(256)S(1)} %convert_element_type.107) | copy-start | bytes 3076
  41.9 28.9 %copy-start.66 = (f32[640]{0:T(1024)}, f32[640]{0:T(1024)S(1)}, u32[]{:S(2)}) copy-start(f32[640]{0:T(1024)S(1)} %convert_element_type.104) | copy-start | bytes 7684
  43.7 31.5 %copy-start.46 = (f32[1536]{0:T(1024)}, f32[1536]{0:T(1024)S(1)}, u32[]{:S(2)}) copy-start(f32[1536]{0:T(1024)S(1)} %subtract_convert_fusion.1) | copy-start | bytes 18436
  66.8 4.0 copy-start.62
  74.0 61.4 %copy-start.5 = (f32[1536,512]{0,1:T(8,128)}, f32[1536,512]{0,1:T(8,128)S(1)}, u32[]{:S(2)}) copy-start(f32[1536,512]{0,1:T(8,128)S(1)} %fusion.116) | copy-start | bytes 9437188
  75.0 4.3 copy-start.43
  79.3 51.7 %copy-start.35 = (bf16[1536,128]{0,1:T(8,128)(2,1)}, bf16[1536,128]{0,1:T(8,128)(2,1)S(1)}, u32[]{:S(2)}) copy-start(bf16[1536,128]{0,1:T(8,128)(2,1)S(1)} %get-tuple-element.126) | copy-start | bytes 1179652
  79.3 8.6 %copy-start.63 = (f32[1536]{0:T(1024)S(1)}, f32[1536]{0:T(1024)}, u32[]{:S(2)}) copy-start(f32[1536]{0:T(1024)} %copy-done.62) | copy-start | bytes 18436
  96.0 7.9 %copy-start.72 = (f32[256]{0:T(256)S(1)}, f32[256]{0:T(256)}, u32[]{:S(2)}) copy-start(f32[256]{0:T(256)} %convert_element_type.109) | copy-start | bytes 3076
  108.5 22.5 %copy-start.21 = (bf16[1536,4,128]{2,0,1:T(8,128)(2,1)}, bf16[1536,4,128]{2,0,1:T(8,128)(2,1)S(1)}, u32[]{:S(2)}) copy-start(bf16[1536,4,128]{2,0,1:T(8,128)(2,1)S(1)} %get-tuple-element.117) | copy-start | bytes 4718596
  108.5 22.5 %copy-start.23 = (bf16[1536,4,128]{2,0,1:T(8,128)(2,1)}, bf16[1536,4,128]{2,0,1:T(8,128)(2,1)S(1)}, u32[]{:S(2)}) copy-start(bf16[1536,4,128]{2,0,1:T(8,128)(2,1)S(1)} %get-tuple-element.118) | copy-start | bytes 4718596
  111.7 4.6 copy-start.1
  122.4 4.7 copy-start
  122.4 4.7 copy-start.56
  127.1 3.9 copy-start.39
  133.6 4.7 copy-start.2
  133.6 4.7 copy-start.60
  141.3 4.9 copy-start.25
  141.3 4.9 copy-start.13
  150.4 10.5 %copy-start.26 = (bf16[1536,640]{0,1:T(8,128)(2,1)}, bf16[1536,640]{0,1:T(8,128)(2,1)S(1)}, u32[]{:S(2)}) copy-start(bf16[1536,640]{0,1:T(8,128)(2,1)S(1)} %multiply_convert_fusion.2) | copy-start | bytes 5898244
  177.7 7.5 %copy-start.15 = (bf16[1536,640]{0,1:T(8,128)(2,1)S(1)}, bf16[1536,640]{0,1:T(8,128)(2,1)}, u32[]{:S(2)}) copy-start(bf16[1536,640]{0,1:T(8,128)(2,1)} %copy.166) | copy-start | bytes 5898244
  177.7 7.5 %copy-start.53 = (f32[640]{0:T(1024)S(1)}, f32[640]{0:T(1024)}, u32[]{:S(2)}) copy-start(f32[640]{0:T(1024)} %convert_element_type.118) | copy-start | bytes 7684
  177.7 7.5 %copy-start.65 = (pred[1536]{0:T(1024)(128)(4,1)S(1)}, pred[1536]{0:T(1024)(128)(4,1)}, u32[]{:S(2)}) copy-start(pred[1536]{0:T(1024)(128)(4,1)} %iota_compare_fusion.4) | copy-start | bytes 4612
  214.6 7.8 %copy-start.77 = (bf16[640,2048]{1,0:T(8,128)(2,1)S(1)}, bf16[640,2048]{1,0:T(8,128)(2,1)}, u32[]{:S(2)}) copy-start(bf16[640,2048]{1,0:T(8,128)(2,1)} %all-gather.12.cloned.1.call-done) | copy-start | bytes 7864324
  214.6 7.8 %copy-start.81 = (bf16[1536,2048]{1,0:T(8,128)(2,1)S(1)}, bf16[1536,2048]{1,0:T(8,128)(2,1)}, u32[]{:S(2)}) copy-start(bf16[1536,2048]{1,0:T(8,128)(2,1)} %get-tuple-element.113) | copy-start | bytes 18874372
  222.4 5.5 copy-start.11
  222.4 5.5 copy-start.16
  231.1 5.4 slice-start
  231.1 5.9 slice-start.1
  233.4 4.8 slice-start.2
  247.0 18.7 %slice-start.3 = ((s8[12582912]{0:T(1024)(128)(4,1)}), s8[4194304]{0:T(1024)(128)(4,1)S(1)}, s32[]{:S(2)}) async-start(s8[12582912]{0:T(1024)(128)(4,1)} %bitcast.153), calls=%async_computation.21 | async-start | bytes 8388608
  247.0 18.7 %slice-start.4 = ((s8[12582912]{0:T(1024)(128)(4,1)}), s8[4194304]{0:T(1024)(128)(4,1)S(1)}, s32[]{:S(2)}) async-start(s8[12582912]{0:T(1024)(128)(4,1)} %bitcast.153), calls=%async_computation.22 | async-start | bytes 8388608
  257.5 8.2 %slice-start.5 = ((s8[12582912]{0:T(1024)(128)(4,1)}), s8[4194304]{0:T(1024)(128)(4,1)S(1)}, s32[]{:S(2)}) async-start(s8[12582912]{0:T(1024)(128)(4,1)} %bitcast.153), calls=%async_computation.23 | async-start | bytes 8388608
  277.1 9.7 %copy-start.22 = (bf16[1536,4,128]{2,0,1:T(8,128)(2,1)S(1)}, bf16[1536,4,128]{2,0,1:T(8,128)(2,1)}, u32[]{:S(2)}) copy-start(bf16[1536,4,128]{2,0,1:T(8,128)(2,1)} %copy-done.21) | copy-start | bytes 4718596
  277.1 9.7 %copy-start.24 = (bf16[1536,4,128]{2,0,1:T(8,128)(2,1)S(1)}, bf16[1536,4,128]{2,0,1:T(8,128)(2,1)}, u32[]{:S(2)}) copy-start(bf16[1536,4,128]{2,0,1:T(8,128)(2,1)} %copy-done.23) | copy-start | bytes 4718596
  292.6 19.1 %slice-start.8 = ((s8[12582912]{0:T(1024)(128)(4,1)}), s8[4194304]{0:T(1024)(128)(4,1)S(1)}, s32[]{:S(2)}) async-start(s8[12582912]{0:T(1024)(128)(4,1)} %bitcast.157), calls=%async_computation.26 | async-start | bytes 8388608
  292.6 19.1 %slice-start.9 = ((s8[12582912]{0:T(1024)(128)(4,1)}), s8[4194304]{0:T(1024)(128)(4,1)S(1)}, s32[]{:S(2)}) async-start(s8[12582912]{0:T(1024)(128)(4,1)} %bitcast.157), calls=%async_computation.27 | async-start | bytes 8388608
  292.6 19.1 %slice-start.10 = ((s8[12582912]{0:T(1024)(128)(4,1)}), s8[4194304]{0:T(1024)(128)(4,1)S(1)}, s32[]{:S(2)}) async-start(s8[12582912]{0:T(1024)(128)(4,1)} %bitcast.157), calls=%async_computation.28 | async-start | bytes 8388608
  317.1 5.6 copy-start.47
  317.1 5.6 copy-start.76
  317.2 8.7 %copy-start.44 = (f32[1536]{0:T(1024)S(1)}, f32[1536]{0:T(1024)}, u32[]{:S(2)}) copy-start(f32[1536]{0:T(1024)} %copy-done.43) | copy-start | bytes 18436
  317.2 8.7 %copy-start.71 = (f32[256]{0:T(256)S(1)}, f32[256]{0:T(256)}, u32[]{:S(2)}) copy-start(f32[256]{0:T(256)} %copy-done.70) | copy-start | bytes 3076
  329.9 7.2 copy-start.36
  329.9 7.2 copy-start.40
  330.0 73.7 %reduce-scatter.11.cloned.1.call-start = ((), (), s32[]{:S(2)}) async-start(), calls=%async_computation.13 | async-start | bytes 2949120 | tf_op jit(solution)/shard_map/reduce_scatter | solution.py:223
  336.7 102.3 %reduce-scatter.7.cloned.1.call-start = ((), (), s32[]{:S(2)}) async-start(), calls=%async_computation.11 | async-start | bytes 2949120 | tf_op jit(solution)/shard_map/reduce_scatter | solution.py:221
  337.2 11.3 %slice-start.11 = ((s8[6291456]{0:T(1024)(128)(4,1)}), s8[4194304]{0:T(1024)(128)(4,1)S(1)}, s32[]{:S(2)}) async-start(s8[6291456]{0:T(1024)(128)(4,1)} %bitcast.159), calls=%async_computation.29 | async-start | bytes 8388608
  342.8 5.7 slice-start.12
  373.8 126.6 %reduce-scatter.17.cloned.1.call-start = ((), (), s32[]{:S(2)}) async-start(), calls=%async_computation.16 | async-start | bytes 5898240 | tf_op jit(solution)/shard_map/reduce_scatter | solution.py:226
  383.2 177.6 %reduce-scatter.13.cloned.1.call-start = ((), (), s32[]{:S(2)}) async-start(), calls=%async_computation.14 | async-start | bytes 5898240 | tf_op jit(solution)/shard_map/reduce_scatter | solution.py:224
  393.4 227.9 %reduce-scatter.15.cloned.1.call-start = ((), (), s32[]{:S(2)}) async-start(), calls=%async_computation.15 | async-start | bytes 5898240 | tf_op jit(solution)/shard_map/reduce_scatter | solution.py:225
  403.6 302.4 %all-reduce.22.cloned.1.call-start = ((), (), s32[]{:S(2)}) async-start(), calls=%async_computation.17 | async-start | bytes 5570560 | tf_op jit(solution)/shard_map/psum | solution.py:234
  626.9 4.9 copy-start.33
  626.9 4.9 copy-start.80
  637.2 5.5 copy-start.68
  637.2 5.5 copy-start.69
  637.2 5.5 copy-start.74
  706.0 9.0 %copy-start.34 = (f32[256,640]{1,0:T(8,128)S(1)}, f32[256,640]{1,0:T(8,128)}, u32[]{:S(2)}) copy-start(f32[256,640]{1,0:T(8,128)} %get-tuple-element.170) | copy-start | bytes 1966084
  (43 other events, 96.3 us)
Sparse Core Ops, SparseCore 0:
  9.7 26.5 all-gather.5
  37.8 27.0 all-gather.7
  66.6 33.1 all-gather.9
  101.3 32.8 all-gather.11
  135.7 32.8 all-gather.13
  330.1 32.0 reduce-scatter.8
  364.4 35.6 reduce-scatter.10
  402.4 36.4 reduce-scatter.6
  441.3 59.0 reduce-scatter.16
  502.5 58.2 reduce-scatter.12
  563.1 58.2 reduce-scatter.14
  625.1 80.8 all-reduce.21
where the time goes:
time: 733 us; the launch traced here: 723 us
  waiting for transfers between devices  247 us (34%)
  matrix products  231 us (32%)
  other arithmetic  81.6 us (11%)
  blocking collectives  74.3 us (10%)
  local copies, waits for them, and re-layouts  70.1 us (10%)
  between operations  18.3 us (2%)
    reduce_scatter x1, waiting for transfers between devices, shards(): lax.psum_scatter(down_grad, 'shard', scatter_dimension=0, tiled=True)  61.4 us
    reduce_scatter x1, waiting for transfers between devices, shards(): lax.psum_scatter(upward_grad, 'shard', scatter_dimension=0, tiled=True)  60.6 us
    reduce_scatter x1, waiting for transfers between devices, shards(): lax.psum_scatter(gate_grad, 'shard', scatter_dimension=0, tiled=True)  60.4 us
    unnamed x219, local copies, waits for them, and re-layouts  53.8 us
    dot_general x6, matrix products, right_dot(): lax.dot_general(left, right, (((1,), (1,)), ((), ())), preferred_element_...  46.9 us
    unnamed x2, blocking collectives  45 us
    dot_general x6, matrix products, left_dot(): lax.dot_general(left, right, (((0,), (0,)), ((), ())), preferred_element_...  44.3 us
    reduce_scatter x1, waiting for transfers between devices, shards(): lax.psum_scatter(query_grad, 'shard', scatter_dimension=0, tiled=True)  35.3 us
  transfers between devices with their start and end apart: 12, of which 5 were waited for; matrix products, arithmetic and copies ran while one was open for 28% of the time, Pallas kernels for 0%

commit v1 on v0

v1 whole, which is shorter than its diff:
```python
import jax
import jax.numpy as jnp
from jax import lax
from jax.sharding import PartitionSpec as P

QH = 4
HD = 256


EPS = 1e-06
THETA = 1000000.0
NEG = -1e30


def normed(value, gain):
    return value * lax.rsqrt(jnp.mean(value * value, axis=-1, keepdims=True) + EPS) * gain


def rotary(position, width):
    freqs = THETA ** (-(jnp.arange(width // 2, dtype=jnp.float32) * 2.0 / width))
    angles = position.astype(jnp.float32)[:, None] * freqs[None, :]
    return (jnp.cos(angles), jnp.sin(angles))


def rotate(value, cosine, sine):
    half = value.shape[-1] // 2
    first = value[..., :half]
    second = value[..., half:]
    return jnp.concatenate(
        [first * cosine - second * sine, second * cosine + first * sine], axis=-1
    )


def layout(seq_lengths, seq_device, device, rows):
    mine = seq_device == device
    lens = jnp.where(mine, seq_lengths, 0)
    ends = jnp.cumsum(lens, dtype=jnp.int32)
    starts = ends - lens
    row_ids = jnp.arange(rows, dtype=jnp.int32)
    begun = mine[None, :] & (starts[None, :] <= row_ids[:, None])
    segment = jnp.sum(begun.astype(jnp.int32), axis=1, dtype=jnp.int32)
    own_start = jnp.max(jnp.where(begun, starts[None, :], 0), axis=1)
    position = row_ids - own_start
    live = row_ids < jnp.sum(lens, dtype=jnp.int32)
    return (segment, position, live)


def left_dot(left, right):
    return lax.dot_general(
        left, right, (((0,), (0,)), ((), ())), preferred_element_type=jnp.float32
    )


def right_dot(left, right):
    return lax.dot_general(
        left, right, (((1,), (1,)), ((), ())), preferred_element_type=jnp.float32
    )


def scatter(grad):
    return lax.psum_scatter(grad, "shard", scatter_dimension=0, tiled=True)


def rep_sum(part, flip):
    size = lax.axis_size("rep")
    if size & (size - 1):
        return lax.psum(part.astype(jnp.float32), "rep")
    steps = [1 << bit for bit in range(size.bit_length() - 1)]
    if flip:
        steps = steps[::-1]
    total = part
    for step in steps:
        pairs = [(peer, peer ^ step) for peer in range(size)]
        other = lax.ppermute(total.astype(jnp.bfloat16), "rep", pairs)
        total = total.astype(jnp.bfloat16).astype(jnp.float32) + other.astype(jnp.float32)
    return total


def permuted_gather(part):
    size = lax.axis_size("shard")
    if size > 8:
        return lax.all_gather(part, "shard", axis=0, tiled=True)
    me = lax.axis_index("shard")
    rows = part.shape[0]
    full = jnp.zeros((size * rows, part.shape[1]), part.dtype)
    full = lax.dynamic_update_slice(full, part, (me * rows, 0))
    for shift in range(1, size):
        piece = lax.ppermute(
            part, "shard", [(peer, (peer + shift) % size) for peer in range(size)]
        )
        owner = lax.rem(me + size - shift, size)
        full = lax.dynamic_update_slice(full, piece, (owner * rows, 0))
    return full


def shards(
    tokens,
    seq_lengths,
    seq_device,
    w_query,
    w_keyval,
    w_project,
    w_gate,
    w_upward,
    w_down,
    gain_input,
    gain_query,
    gain_key,
    gain_attend,
    gain_before,
    gain_after,
    cotangent,
):
    rows = tokens.shape[0]
    device = lax.axis_index("shard") * lax.axis_size("rep") + lax.axis_index("rep")
    segment, position, live = layout(seq_lengths, seq_device, device, rows)
    cosine, sine = rotary(position, HD)
    n_shard = lax.axis_size("shard")
    d_model = w_query.shape[0] * n_shard
    part = w_query.shape[0]

    def column(gain):
        return jnp.pad(gain, (0, part - gain.shape[0]))[:, None]

    gain_cols = jnp.concatenate(
        [column(g) for g in (gain_input, gain_query, gain_key, gain_attend, gain_before, gain_after)]
        + [jnp.zeros((part, 122), jnp.bfloat16)],
        axis=1,
    )
    pack = lax.all_gather(
        jnp.concatenate([w_query, w_keyval, gain_cols], axis=1), "shard", axis=0, tiled=True
    )
    pack, project_part = lax.optimization_barrier((pack, w_project))
    project_full = permuted_gather(project_part)
    q_cols = w_query.shape[1]
    kv_cols = w_keyval.shape[1]
    qkv_full = pack[:, : q_cols + kv_cols]
    gains = pack[:, q_cols + kv_cols : q_cols + kv_cols + 6].T
    input_full, attend_full, before_full, after_full = gains[0], gains[3], gains[4], gains[5]
    head_part = gain_query.shape[0]
    qgain_full = gains[1].reshape(n_shard, part)[:, :head_part].reshape(HD)
    kgain_full = gains[2].reshape(n_shard, part)[:, :head_part].reshape(HD)
    query_full = qkv_full[:, :q_cols]
    keyval_full = qkv_full[:, q_cols:]
    gate_full = lax.all_gather(w_gate, "shard", axis=0, tiled=True)
    upward_full = lax.all_gather(w_upward, "shard", axis=0, tiled=True)
    down_full = lax.all_gather(w_down, "shard", axis=0, tiled=True)
    x_rows = tokens.astype(jnp.float32)
    h_value, back_input = jax.vjp(normed, x_rows, input_full.astype(jnp.float32))
    h_low = h_value.astype(jnp.bfloat16)
    q_raw = jnp.dot(h_low, query_full, preferred_element_type=jnp.float32).reshape(rows, QH, HD)
    kv_raw = jnp.dot(h_low, keyval_full, preferred_element_type=jnp.float32)

    def query_side(value, gain):
        return rotate(normed(value, gain), cosine[:, None, :], sine[:, None, :])

    def key_side(value, gain):
        return rotate(normed(value, gain), cosine, sine)

    q_rot, back_query = jax.vjp(query_side, q_raw, qgain_full.astype(jnp.float32))
    k_rot, back_key = jax.vjp(key_side, kv_raw[:, :HD], kgain_full.astype(jnp.float32))
    q_low = q_rot.astype(jnp.bfloat16)
    k_low = k_rot.astype(jnp.bfloat16)
    v_low = kv_raw[:, HD:].astype(jnp.bfloat16)
    block = rows // 3
    scale = HD ** (-0.5)
    row_ids = jnp.arange(rows, dtype=jnp.int32)

    def block_scores(index):
        q_block = q_low[index * block : (index + 1) * block]
        seen = (index + 1) * block
        raw = (
            jnp.einsum("qhd,kd->hqk", q_block, k_low[:seen], preferred_element_type=jnp.float32)
            * scale
        )
        seg_block = segment[index * block : (index + 1) * block]
        row_block = row_ids[index * block : (index + 1) * block]
        allowed = (seg_block[:, None] == segment[None, :seen]) & (
            row_ids[None, :seen] <= row_block[:, None]
        )
        return (jnp.where(allowed[None], raw, NEG), q_block)

    out_parts = []
    lse_parts = []
    for index in range(3):
        logits, q_block = block_scores(index)
        peak = jnp.max(logits, axis=-1, keepdims=True)
        expo = jnp.exp(logits - peak)
        total = jnp.sum(expo, axis=-1, keepdims=True)
        probs = expo / total
        out_parts.append(
            jnp.einsum(
                "hqk,kd->qhd", probs.astype(jnp.bfloat16), v_low[: (index + 1) * block],
                preferred_element_type=jnp.float32,
            )
        )
        lse_parts.append(peak + jnp.log(total))
    attended = jnp.concatenate(out_parts, axis=0).reshape(rows, QH * HD).astype(jnp.bfloat16)
    branch = jnp.dot(attended, project_full, preferred_element_type=jnp.float32)
    branch_normed, back_attend = jax.vjp(normed, branch, attend_full.astype(jnp.float32))
    x_mid = x_rows + branch_normed
    h_two, back_before = jax.vjp(normed, x_mid, before_full.astype(jnp.float32))
    h_two_low = h_two.astype(jnp.bfloat16)
    gate = jnp.dot(h_two_low, gate_full, preferred_element_type=jnp.float32)
    upper = jnp.dot(h_two_low, upward_full, preferred_element_type=jnp.float32)
    hidden, back_glu = jax.vjp(
        lambda g_val, u_val: jax.nn.gelu(g_val, approximate=True) * u_val, gate, upper
    )
    hidden_low = hidden.astype(jnp.bfloat16)
    ffn = jnp.dot(hidden_low, down_full, preferred_element_type=jnp.float32)
    ffn_normed, back_after = jax.vjp(normed, ffn, after_full.astype(jnp.float32))
    activations = (x_mid + ffn_normed).astype(jnp.bfloat16)
    upstream = jnp.where(live[:, None], cotangent.astype(jnp.float32), jnp.float32(0.0))
    d_ffn, aftergain_grad = back_after(upstream)
    d_ffn_low = d_ffn.astype(jnp.bfloat16)
    down_grad = left_dot(hidden_low, d_ffn_low).astype(jnp.bfloat16)
    down_grad, d_ffn_low = lax.optimization_barrier((down_grad, d_ffn_low))
    down_share = scatter(down_grad)
    d_hidden = right_dot(d_ffn_low, down_full)
    d_gate, d_up = back_glu(d_hidden)
    d_gate_low = d_gate.astype(jnp.bfloat16)
    d_up_low = d_up.astype(jnp.bfloat16)
    gate_grad = left_dot(h_two_low, d_gate_low).astype(jnp.bfloat16)
    upward_grad = left_dot(h_two_low, d_up_low).astype(jnp.bfloat16)
    gate_grad, upward_grad, d_gate_low, d_up_low = lax.optimization_barrier(
        (gate_grad, upward_grad, d_gate_low, d_up_low)
    )
    gate_share = scatter(gate_grad)
    upward_share = scatter(upward_grad)
    d_h_two = right_dot(d_gate_low, gate_full) + right_dot(d_up_low, upward_full)
    d_mid_part, beforegain_grad = back_before(d_h_two)
    d_mid = upstream + d_mid_part
    d_branch, attendgain_grad = back_attend(d_mid)
    d_branch_low = d_branch.astype(jnp.bfloat16)
    project_grad = left_dot(attended, d_branch_low).astype(jnp.bfloat16)
    project_grad, d_branch_low = lax.optimization_barrier((project_grad, d_branch_low))
    project_share = scatter(project_grad)
    d_attended = right_dot(d_branch_low, project_full).reshape(rows, QH, HD).astype(jnp.bfloat16)
    down_share, d_attended = lax.optimization_barrier((down_share, d_attended))
    dq_parts = []
    d_keys = jnp.zeros((rows, HD), jnp.float32)
    d_values = jnp.zeros((rows, HD), jnp.float32)
    for index in range(3):
        logits, q_block = block_scores(index)
        probs = jnp.exp(logits - lse_parts[index])
        d_block = d_attended[index * block : (index + 1) * block]
        seen = (index + 1) * block
        d_probs = jnp.einsum(
            "qhd,kd->hqk", d_block, v_low[:seen], preferred_element_type=jnp.float32
        )
        spread = jnp.sum(probs * d_probs, axis=-1, keepdims=True)
        d_logits = (probs * (d_probs - spread)).astype(jnp.bfloat16)
        dq_parts.append(
            jnp.einsum(
                "hqk,kd->qhd", d_logits, k_low[:seen], preferred_element_type=jnp.float32
            )
            * scale
        )
        rest = ((0, rows - seen), (0, 0))
        d_keys = d_keys + jnp.pad(
            jnp.einsum("hqk,qhd->kd", d_logits, q_block, preferred_element_type=jnp.float32)
            * scale,
            rest,
        )
        d_values = d_values + jnp.pad(
            jnp.einsum(
                "hqk,qhd->kd",
                probs.astype(jnp.bfloat16),
                d_block,
                preferred_element_type=jnp.float32,
            ),
            rest,
        )
    sum_down = rep_sum(down_share, False)
    sum_down, gate_share, upward_share, d_keys = lax.optimization_barrier(
        (sum_down, gate_share, upward_share, d_keys)
    )
    sum_gate = rep_sum(gate_share, True)
    sum_upward = rep_sum(upward_share, False)
    d_queries = jnp.concatenate(dq_parts, axis=0)
    d_q_raw, querygain_grad = back_query(d_queries)
    d_k_raw, keygain_grad = back_key(d_keys)
    d_q_low = d_q_raw.reshape(rows, QH * HD).astype(jnp.bfloat16)
    d_kv_low = jnp.concatenate([d_k_raw, d_values], axis=1).astype(jnp.bfloat16)
    d_qkv_low = jnp.concatenate([d_q_low, d_kv_low], axis=1)
    qkv_grad = left_dot(h_low, d_qkv_low).astype(jnp.bfloat16)

    def spread_rows(grad):
        return jnp.pad(grad.reshape(n_shard, -1), ((0, 0), (0, part - head_part))).reshape(d_model)

    grad_cols = jnp.stack(
        [
            spread_rows(querygain_grad),
            spread_rows(keygain_grad),
            attendgain_grad,
            beforegain_grad,
            aftergain_grad,
        ],
        axis=1,
    ).astype(jnp.bfloat16)
    grad_pack = jnp.concatenate(
        [qkv_grad, grad_cols, jnp.zeros((d_model, 123), jnp.bfloat16)], axis=1
    )
    grad_pack, d_qkv_low = lax.optimization_barrier((grad_pack, d_qkv_low))
    sum_gate, sum_upward, project_share, grad_pack = lax.optimization_barrier(
        (sum_gate, sum_upward, project_share, grad_pack)
    )
    pack_share = scatter(grad_pack)
    d_h = right_dot(d_qkv_low, qkv_full)
    d_input_part = back_input(d_h)[0]
    input_grad = d_mid + d_input_part
    sum_project = rep_sum(project_share, True)
    sum_pack = rep_sum(pack_share, False)
    sum_query = sum_pack[:, :q_cols]
    sum_keyval = sum_pack[:, q_cols : q_cols + kv_cols]
    sum_gains = sum_pack[:, q_cols + kv_cols : q_cols + kv_cols + 5].T
    sum_qgain, sum_kgain = sum_gains[0, :head_part], sum_gains[1, :head_part]
    sum_attend, sum_before, sum_after = sum_gains[2], sum_gains[3], sum_gains[4]
    sum_input = (
        jnp.sum(sum_query * w_query.astype(jnp.float32), axis=1)
        + jnp.sum(sum_keyval * w_keyval.astype(jnp.float32), axis=1)
    ) / gain_input.astype(jnp.float32)
    return (
        activations,
        input_grad,
        sum_query,
        sum_keyval,
        sum_project,
        sum_gate,
        sum_upward,
        sum_down,
        sum_input,
        sum_qgain,
        sum_kgain,
        sum_attend,
        sum_before,
        sum_after,
    )


def solution(mesh):
    return jax.shard_map(
        shards,
        mesh=mesh,
        in_specs=(
            P(("shard", "rep"), None),
            P(),
            P(),
            P("shard", None),
            P("shard", None),
            P("shard", None),
            P("shard", None),
            P("shard", None),
            P("shard", None),
            P("shard"),
            P("shard"),
            P("shard"),
            P("shard"),
            P("shard"),
            P("shard"),
            P(("shard", "rep"), None),
        ),
        out_specs=(
            P(("shard", "rep"), None),
            P(("shard", "rep"), None),
            P("shard", None),
            P("shard", None),
            P("shard", None),
            P("shard", None),
            P("shard", None),
            P("shard", None),
            P("shard"),
            P("shard"),
            P("shard"),
            P("shard"),
            P("shard"),
            P("shard"),
        ),
        check_vma=False,
    )
```

time: 733 us -> 484 us (0.66)
  waiting for transfers between devices: 247 us -> 79.4 us
  blocking collectives: 74.3 us -> 0 us
  matrix products: 231 us -> 195 us
  starting transfers between devices: 0.88 us -> 20.7 us
  other arithmetic: 81.6 us -> 90.8 us
    reduce_scatter x6 -> x5, waiting for transfers between devices: 218 us -> 21.1 us  [scatter(): return lax.psum_scatter(grad, 'shard', scatter_dimension=0, tiled=True)]
    unnamed x2 -> x0, blocking collectives: 45 us -> none
    ppermute x0 -> x17, waiting for transfers between devices: none -> 28.8 us  [the longest x10 21.7 us: rep_sum(): other = lax.ppermute(total.astype(jnp.bfloat16), 'rep', pairs)]
    all_gather x5 -> x4, waiting for transfers between devices: 0.05 us -> 26.9 us  [the longest x1 13.7 us: shards(): lax.all_gather(jnp.concatenate([w_query, w_keyval, gain_cols], axis=1), '...]
    psum x1 -> x0, waiting for transfers between devices: 25.8 us -> none  [shards(): lax.psum((all_shares[0], all_shares[1], all_shares[2], all_shares[3], all...]
    unnamed x219 -> x198, local copies, waits for them, and re-layouts: 53.8 us -> 29.4 us
    ppermute x0 -> x17, starting transfers between devices: none -> 20.4 us  [the longest x10 11.5 us: rep_sum(): other = lax.ppermute(total.astype(jnp.bfloat16), 'rep', pairs)]
    all_gather x1 -> x0, blocking collectives: 18.5 us -> none  [shards(): lax.all_gather(w_keyval, 'shard', axis=0, tiled=True)]
  transfers between devices with their start and end apart: 12 -> 26, of which waited for: 5 -> 10; matrix products, arithmetic and copies ran while one was open for 28% -> 67% of each run, Pallas kernels for 0% -> 0%
where the time goes in v1:
time: 484 us; the launch traced here: 476 us
  matrix products  195 us (40%)
  other arithmetic  90.8 us (19%)
  waiting for transfers between devices  79.4 us (16%)
  local copies, waits for them, and re-layouts  74.6 us (15%)
  starting transfers between devices  20.7 us (4%)
  between operations  15.6 us (3%)
    dot_general x5, matrix products, right_dot(): lax.dot_general(left, right, (((1,), (1,)), ((), ())), preferred_element_...  51.6 us
    dot_general x5, matrix products, left_dot(): lax.dot_general(left, right, (((0,), (0,)), ((), ())), preferred_element_...  35.1 us
    unnamed x198, local copies, waits for them, and re-layouts  29.4 us
    ppermute x10, waiting for transfers between devices, rep_sum(): other = lax.ppermute(total.astype(jnp.bfloat16), 'rep', pairs)  21.7 us
    reduce_scatter x5, waiting for transfers between devices, scatter(): return lax.psum_scatter(grad, 'shard', scatter_dimension=0, tiled=True)  21.1 us
    dot_general x1, matrix products, shards(): upper = jnp.dot(h_two_low, upward_full, preferred_element_type=jnp.float32)  16.8 us
    dot_general x3, matrix products, shards(): jnp.einsum('qhd,kd->hqk', d_block, v_low[:seen], preferred_element_type=j...  16.8 us
    convert_element_type x3, other arithmetic, shards(): d_logits = (probs * (d_probs - spread)).astype(jnp.bfloat16)  13.7 us
  transfers between devices with their start and end apart: 26, of which 10 were waited for; matrix products, arithmetic and copies ran while one was open for 67% of the time, Pallas kernels for 0%

profile of v1, /device:TPU:0, one launch (start us, length us, event | category | flops | bytes accessed | tf_op | source)
XLA Modules:
  0.0 476.5 jit_solution(9208696607264038089)
XLA Ops:
  19.5 2.7 copy.128
  22.7 4.3 copy.145
  32.2 13.7 %all-gather.5.cloned.1.call-done = bf16[640,1664]{1,0:T(8,128)(2,1)} async-done(((bf16[80,1664]{1,0:T(8,128)(2,1)}), bf16[640,1664]{1,0:T(8,128)(2,1)}) %all-gather.5.cloned.1.call-update) | async-done | bytes 2129936 | tf_op jit(solution)/shard_map/all_gather | solution.py:130
  48.7 6.7 %multiply_reduce_fusion.2 = (f32[1536,4]{0,1:T(4,128)}, f32[1536,1024]{0,1:T(8,128)}) fusion(bf16[640,1664]{1,0:T(8,128)(2,1)} %all-gather.5.cloned.1.call-done, bf16[1536,640]{0,1:T(8,128)(2,1)S(1)} %copy.128, f32[640]{0:T(1024)S(1)} %get-tuple-element.113, f32[1536]{0:T(1024)S(1)} %fusion.115), kind=kOutput, calls=%fused_computation.47 | convolution fusion | flops 2020337664 | bytes 9601536 | tf_op jit(solution)/shard_map/dot_general | solution.py:151
  55.3 4.3 fusion.139
  62.2 2.8 collective-permute-start.3
  65.2 6.5 %copy.136 = f32[1536,4,256]{2,0,1:T(8,128)} copy(f32[1536,4,256]{0,2,1:T(8,128)} %bitcast.171) | data formatting | bytes 12582912 | tf_op jit(solution)/shard_map/reshape | solution.py:151
  78.4 4.8 %multiply_cosine_fusion = (f32[1536,128]{0,1:T(8,128)}, f32[1536,128]{0,1:T(8,128)}, bf16[1536,128]{0,1:T(8,128)(2,1)}, bf16[1536,128]{0,1:T(8,128)(2,1)}) fusion(f32[128]{0:T(128)} %negate_power_fusion, f32[1536]{0:T(1024)S(1)} %subtract_convert_fusion.1, f32[1536,256]{0,1:T(8,128)S(1)} %multiply_multiply_fusion.4), kind=kLoop, calls=%fused_computation.145 | loop fusion | flops 1769472 | bytes 3938816 | tf_op jit(solution)/shard_map/cos | solution.py:22
  83.2 2.3 copy.138
  85.5 2.3 copy.137
  87.8 3.5 multiply_multiply_fusion.3
  92.8 2.7 fusion.138
  95.5 4.6 fusion.140
  102.6 2.8 fusion.68
  113.2 2.1 collective-permute-start.5
  121.3 7.0 %collective-permute-done.5 = bf16[128,640]{1,0:T(8,128)(2,1)S(1)} collective-permute-done((bf16[128,640]{1,0:T(8,128)(2,1)}, bf16[128,640]{1,0:T(8,128)(2,1)S(1)}, u32[]{:S(2)}, u32[]{:S(2)}) %collective-permute-start.5) | collective-permute-done | bytes 163872 | tf_op jit(solution)/shard_map/ppermute | solution.py:88
  128.6 2.4 multiply_reduce_fusion.11
  132.9 1.9 copy-done.5
  135.3 10.4 %fusion.142 = f32[1536,2048]{1,0:T(8,128)} fusion(bf16[1536,640]{0,1:T(8,128)(2,1)S(1)} %multiply_convert_fusion.2, bf16[640,2048]{1,0:T(8,128)(2,1)} %all-gather.7.cloned.1.call-done), kind=kOutput, calls=%fused_computation.274 | convolution fusion | flops 4026531840 | bytes 17170432 | tf_op jit(solution)/shard_map/dot_general | solution.py:204
  145.7 16.8 %multiply_convert_fusion.1 = (bf16[1536,2048]{1,0:T(8,128)(2,1)}, f32[1536,2048]{1,0:T(8,128)}) fusion(f32[1536,2048]{1,0:T(8,128)} %fusion.142, bf16[1536,640]{0,1:T(8,128)(2,1)S(1)} %multiply_convert_fusion.2, bf16[640,2048]{1,0:T(8,128)(2,1)} %all-gather.9.cloned.1.call-done), kind=kOutput, calls=%fused_computation.17 | convolution fusion | flops 4057989120 | bytes 36044800 | tf_op jit(solution)/shard_map/dot_general | solution.py:205
  162.4 13.2 %all-gather.11.cloned.1.call-done = bf16[2048,640]{1,0:T(8,128)(2,1)} async-done(((bf16[256,640]{1,0:T(8,128)(2,1)}), bf16[2048,640]{1,0:T(8,128)(2,1)}) %all-gather.11.cloned.1.call-update) | async-done | bytes 2621456 | tf_op jit(solution)/shard_map/all_gather | solution.py:147
  175.6 7.5 %multiply_reduce_fusion.9 = (f32[1536]{0:T(1024)S(1)}, f32[1536,640]{0,1:T(8,128)S(1)}) fusion(bf16[1536,2048]{1,0:T(8,128)(2,1)} %get-tuple-element.163, bf16[2048,640]{1,0:T(8,128)(2,1)} %all-gather.11.cloned.1.call-done), kind=kOutput, calls=%fused_computation.84 | convolution fusion | flops 4028496384 | bytes 12851200 | tf_op jit(solution)/shard_map/dot_general | solution.py:210
  185.2 2.8 fusion.29
  189.3 6.6 %convolution_convert_fusion.3 = bf16[2048,640]{1,0:T(8,128)(2,1)} fusion(bf16[1536,2048]{1,0:T(8,128)(2,1)S(1)} %bitcast.180, bf16[1536,640]{0,1:T(8,128)(2,1)S(1)} %get-tuple-element.38), kind=kOutput, calls=%fused_computation.98 | convolution fusion | flops 4027842560 | bytes 10878976 | tf_op jit(solution)/shard_map/dot_general | solution.py:49
  195.9 24.5 %multiply_convert_fusion = (bf16[1536,2048]{1,0:T(8,128)(2,1)}, bf16[1536,2048]{1,0:T(8,128)(2,1)}) fusion(f32[1536,2048]{1,0:T(8,128)} %fusion.142, f32[1536,2048]{1,0:T(8,128)} %get-tuple-element.164, bf16[1536,640]{0,1:T(8,128)(2,1)} %copy-done.33, bf16[2048,640]{1,0:T(8,128)(2,1)} %all-gather.11.cloned.1.call-done), kind=kOutput, calls=%fused_computation.16 | convolution fusion | flops 4102029312 | bytes 42336256 | tf_op jit(solution)/shard_map/dot_general | solution.py:55
  220.4 9.2 %convolution_convert_fusion.2 = bf16[640,2048]{1,0:T(8,128)(2,1)} fusion(bf16[1536,640]{0,1:T(8,128)(2,1)} %copy-done.32, bf16[1536,2048]{1,0:T(8,128)(2,1)} %get-tuple-element.39), kind=kOutput, calls=%fused_computation.97 | convolution fusion | flops 4027842560 | bytes 10878976 | tf_op jit(solution)/shard_map/dot_general | solution.py:49
  229.6 9.3 %convolution_convert_fusion.1 = bf16[640,2048]{1,0:T(8,128)(2,1)} fusion(bf16[1536,640]{0,1:T(8,128)(2,1)} %copy-done.32, bf16[1536,2048]{1,0:T(8,128)(2,1)} %get-tuple-element.40), kind=kOutput, calls=%fused_computation.96 | convolution fusion | flops 4027842560 | bytes 10878976 | tf_op jit(solution)/shard_map/dot_general | solution.py:49
  239.8 7.6 %fusion.143 = f32[1536,640]{0,1:T(8,128)S(1)} fusion(bf16[1536,2048]{1,0:T(8,128)(2,1)} %get-tuple-element.39, bf16[640,2048]{1,0:T(8,128)(2,1)} %all-gather.7.cloned.1.call-done), kind=kOutput, calls=%fused_computation.275 | convolution fusion | flops 4026531840 | bytes 12845056 | tf_op jit(solution)/shard_map/dot_general | solution.py:55
  247.4 7.3 %multiply_reduce_fusion.4 = (bf16[640]{0:T(1024)(128)(2,1)S(1)}, f32[1536]{0:T(1024)S(1)}, f32[1536,640]{0,1:T(8,128)S(1)}) fusion(f32[1536,640]{0,1:T(8,128)S(1)} %copy-done.7, f32[1536]{0:T(1024)S(1)} %fusion.118, f32[640]{0:T(1024)S(1)} %copy-done.67, f32[1536,640]{0,1:T(8,128)S(1)} %fusion.143, bf16[1536,2048]{1,0:T(8,128)(2,1)} %get-tuple-element.40, ...), kind=kOutput, calls=%fused_computation.76 | convolution fusion | flops 4033411072 | bytes 20725504 | tf_op jit(solution)/shard_map/dot_general | solution.py:55
  254.8 2.4 multiply_reduce_fusion.5
  260.5 3.8 convolution_convert_fusion.5
  266.7 4.0 convolution_convert_fusion
  270.9 3.6 copy.148
  274.5 6.9 %fusion.64 = f32[1024,256]{0,1:T(8,128)} fusion(f32[4,512,1024]{1,2,0:T(8,128)} %get-tuple-element.158, f32[4,512]{1,0:T(4,128)S(1)} %log_add_fusion.1, bf16[1536,4,256]{2,0,1:T(8,128)(2,1)S(1)} %copy.148), kind=kOutput, calls=%fused_computation.135 | convolution fusion | flops 1077936128 | bytes 10493952 | tf_op jit(solution)/shard_map/hqk,qhd->kd/dot_general | solution.py:266
  281.4 7.6 %fusion.12 = (f32[4,512]{1,0:T(4,128)S(1)}, f32[1024,512,4]{1,0,2:T(8,128)}) fusion(f32[4,512,1024]{1,2,0:T(8,128)} %get-tuple-element.158, f32[4,512]{1,0:T(4,128)S(1)} %log_add_fusion.1, bf16[1536,4,256]{2,0,1:T(8,128)(2,1)S(1)} %copy.148, bf16[1536,512]{0,1:T(8,128)(2,1)S(1)} %copy-done.18), kind=kOutput, calls=%fused_computation.26 | convolution fusion | flops 1080031232 | bytes 18366464 | tf_op jit(solution)/shard_map/qhd,kd->hqk/dot_general | solution.py:248
  290.8 3.0 fusion.24
  295.2 6.2 %fusion.7 = (f32[4,512]{1,0:T(4,128)S(1)}, f32[1536,512,4]{1,0,2:T(8,128)}) fusion(f32[4,512,1536]{1,2,0:T(8,128)S(1)} %bitcast.162, f32[4,512]{1,0:T(4,128)S(1)} %log_add_fusion, bf16[1536,4,256]{2,0,1:T(8,128)(2,1)S(1)} %copy.148, bf16[1536,512]{0,1:T(8,128)(2,1)S(1)} %copy-done.18), kind=kOutput, calls=%fused_computation.11 | convolution fusion | flops 1620047872 | bytes 27017216 | tf_op jit(solution)/shard_map/qhd,kd->hqk/dot_general | solution.py:248
  301.4 7.9 %fusion.9 = bf16[4,512,1536]{1,2,0:T(8,128)(2,1)S(1)} fusion(f32[1536,512,4]{1,0,2:T(8,128)} %get-tuple-element.169, f32[4,512,1536]{1,2,0:T(8,128)S(1)} %bitcast.162, f32[4,512]{1,0:T(4,128)S(1)} %get-tuple-element.168, f32[4,512]{1,0:T(4,128)S(1)} %log_add_fusion), kind=kLoop, calls=%fused_computation.13 | loop fusion | flops 12582912 | bytes 31473664 | tf_op jit(solution)/shard_map/convert_element_type | solution.py:252
  309.3 5.2 %multiply_bitcast_fusion = f32[512,4,256]{2,0,1:T(8,128)} fusion(bf16[4,512,1536]{1,2,0:T(8,128)(2,1)S(1)} %fusion.9, bf16[1536,128]{0,1:T(8,128)(2,1)S(1)} %copy-done.36, bf16[1536,128]{0,1:T(8,128)(2,1)} %get-tuple-element.147), kind=kOutput, calls=%fused_computation.115 | convolution fusion | flops 1612709888 | bytes 9175040 | tf_op jit(solution)/shard_map/hqk,kd->qhd/dot_general | solution.py:254
  314.6 4.6 fusion.14
  319.2 3.1 multiply_bitcast_fusion.1
  327.2 5.5 %pad_maximum_fusion = f32[1536,4,256]{2,0,1:T(8,128)} fusion(f32[512,4,256]{2,0,1:T(8,128)} %multiply_bitcast_fusion, f32[512,4,256]{2,0,1:T(8,128)} %multiply_bitcast_fusion.1, f32[512,4,256]{2,0,1:T(8,128)S(1)} %multiply_bitcast_fusion.2), kind=kLoop, calls=%fused_computation.42 | loop fusion | flops 3145728 | bytes 12582912 | tf_op jit(solution)/shard_map/concatenate | solution.py:280
  332.7 4.2 multiply_add_fusion.1
  337.0 2.4 multiply_reduce_fusion
  339.5 3.9 fusion.17
  343.4 3.4 fusion.49
  346.9 2.3 fusion.67
  349.2 5.0 %copy.162 = bf16[1536,4,256]{0,2,1:T(8,128)(2,1)} copy(bf16[1536,4,256]{2,0,1:T(8,128)(2,1)} %fusion.17) | data formatting | bytes 6291456 | tf_op jit(solution)/shard_map/convert_element_type | solution.py:283
  354.5 2.1 fusion.74
  359.4 4.6 fusion.45
  364.1 3.4 collective-permute-done.8
  368.4 3.1 fusion.99
  371.5 2.1 multiply_reduce_fusion.12
  376.9 6.2 %convolution_convert_fusion.4 = bf16[640,1536]{1,0:T(8,128)(2,1)} fusion(bf16[1536,640]{0,1:T(8,128)(2,1)S(1)} %copy-done.4, f32[640]{0:T(1024)S(1)} %copy-done.65, f32[1536]{0:T(1024)S(1)} %copy-done.53, bf16[1536,256]{0,1:T(8,128)(2,1)S(1)} %fusion.49, bf16[1536,256]{0,1:T(8,128)(2,1)S(1)} %fusion.58, bf16[1536,1024]{0,1:T(8,128)(2,1)S(1)} %bitcast.169), kind=kOutput, calls=%fused_computation.99 | convolution fusion | flops 3038969856 | bytes 8659456 | tf_op jit(solution)/shard_map/dot_general | solution.py:49
  383.1 2.4 pad_maximum_fusion.1
  385.9 4.6 concatenate.34
  393.8 7.4 %collective-permute-done.11 = bf16[80,2048]{1,0:T(8,128)(2,1)S(1)} collective-permute-done((bf16[80,2048]{1,0:T(8,128)(2,1)S(1)}, bf16[80,2048]{1,0:T(8,128)(2,1)S(1)}, u32[]{:S(2)}, u32[]{:S(2)}) %collective-permute-start.11) | collective-permute-done | bytes 327712 | tf_op jit(solution)/shard_map/ppermute | solution.py:74
  401.9 4.0 collective-permute-done.10
  409.3 4.2 copy.177
  413.6 8.1 %fusion.36 = (f32[1536]{0:T(1024)S(1)}, f32[1536,640]{0,1:T(8,128)}) fusion(bf16[1536,640]{0,1:T(8,128)(2,1)S(1)} %copy-done.4, f32[640]{0:T(1024)S(1)} %copy-done.65, bf16[1536,1536]{0,1:T(8,128)(2,1)} %pad_maximum_fusion.1, bf16[640,1664]{1,0:T(8,128)(2,1)} %all-gather.5.cloned.1.call-done), kind=kOutput, calls=%fused_computation.74 | convolution fusion | flops 3023829504 | bytes 12591616 | tf_op jit(solution)/shard_map/dot_general | solution.py:55
  422.5 21.0 %reduce-scatter.14.cloned.1.call-done = bf16[80,1664]{1,0:T(8,128)(2,1)} async-done(((bf16[640,1664]{1,0:T(8,128)(2,1)}), bf16[80,1664]{1,0:T(8,128)(2,1)}) %reduce-scatter.14.cloned.1.call-update) | async-done | bytes 266256 | tf_op jit(solution)/shard_map/reduce_scatter | solution.py:61
  445.7 5.3 %collective-permute-done.13 = bf16[80,1664]{1,0:T(8,128)(2,1)S(1)} collective-permute-done((bf16[80,1664]{1,0:T(8,128)(2,1)}, bf16[80,1664]{1,0:T(8,128)(2,1)S(1)}, u32[]{:S(2)}, u32[]{:S(2)}) %collective-permute-start.13) | collective-permute-done | bytes 266272 | tf_op jit(solution)/shard_map/ppermute | solution.py:74
  453.3 6.4 %fusion.32 = f32[1536,640]{0,1:T(8,128)} fusion(f32[1536,640]{0,1:T(8,128)} %copy-done.8, bf16[1536,640]{0,1:T(8,128)(2,1)S(1)} %copy-done.4, f32[1536,640]{0,1:T(8,128)} %get-tuple-element.175, f32[1536]{0:T(1024)S(1)} %multiply_multiply_fusion.6, f32[640]{0:T(1024)S(1)} %copy-done.65, f32[1536]{0:T(1024)S(1)} %copy-done.53), kind=kLoop, calls=%fused_computation.70 | loop fusion | flops 6881280 | bytes 13777408 | tf_op jit(solution)/shard_map/add | solution.py:311
  459.7 5.5 %copy.178 = f32[1536,640]{1,0:T(8,128)} copy(f32[1536,640]{0,1:T(8,128)} %fusion.32) | data formatting | bytes 7864320
  (355 shorter events, 93.0 us)
Async XLA Ops:
  7.2 38.7 %all-gather.5.cloned.1.call-start = ((), (), s32[]{:S(2)}) async-start(), calls=%async_computation.5 | async-start | bytes 2396160 | tf_op jit(solution)/shard_map/all_gather | solution.py:130
  13.7 121.6 %all-gather.7.cloned.1.call-start = ((), (), s32[]{:S(2)}) async-start(), calls=%async_computation.6 | async-start | bytes 2949120 | tf_op jit(solution)/shard_map/all_gather | solution.py:145
  14.4 131.2 %all-gather.9.cloned.1.call-start = ((), (), s32[]{:S(2)}) async-start(), calls=%async_computation.7 | async-start | bytes 2949120 | tf_op jit(solution)/shard_map/all_gather | solution.py:146
  15.2 160.4 %all-gather.11.cloned.1.call-start = ((), (), s32[]{:S(2)}) async-start(), calls=%async_computation.8 | async-start | bytes 2949120 | tf_op jit(solution)/shard_map/all_gather | solution.py:147
  15.7 255.1 %reduce-scatter.6.cloned.1.call-start = ((), (), s32[]{:S(2)}) async-start(), calls=%async_computation.9 | async-start | bytes 2949120 | tf_op jit(solution)/shard_map/reduce_scatter | solution.py:61
  22.2 108.7 %copy-start.3 = (bf16[1536,640]{0,1:T(8,128)(2,1)}, bf16[1536,640]{0,1:T(8,128)(2,1)S(1)}, u32[]{:S(2)}) copy-start(bf16[1536,640]{0,1:T(8,128)(2,1)S(1)} %copy.128) | copy-start | bytes 5898244
  22.7 26.0 %copy-start.60 = (f32[1536]{0:T(1024)}, f32[1536]{0:T(1024)S(1)}, u32[]{:S(2)}) copy-start(f32[1536]{0:T(1024)S(1)} %fusion.33) | copy-start | bytes 18436
  22.7 32.6 %copy-start.52 = (f32[1536]{0:T(1024)}, f32[1536]{0:T(1024)S(1)}, u32[]{:S(2)}) copy-start(f32[1536]{0:T(1024)S(1)} %fusion.115) | copy-start | bytes 18436
  22.7 55.7 %copy-start.58 = (f32[1536]{0:T(1024)}, f32[1536]{0:T(1024)S(1)}, u32[]{:S(2)}) copy-start(f32[1536]{0:T(1024)S(1)} %subtract_convert_fusion.1) | copy-start | bytes 18436
  47.8 7.5 %copy-start.64 = (f32[640]{0:T(1024)}, f32[640]{0:T(1024)S(1)}, u32[]{:S(2)}) copy-start(f32[640]{0:T(1024)S(1)} %get-tuple-element.113) | copy-start | bytes 7684
  59.6 50.7 %copy-start.17 = (bf16[1536,512]{0,1:T(8,128)(2,1)}, bf16[1536,512]{0,1:T(8,128)(2,1)S(1)}, u32[]{:S(2)}) copy-start(bf16[1536,512]{0,1:T(8,128)(2,1)S(1)} %get-tuple-element.155) | copy-start | bytes 4718596
  59.6 53.5 %collective-permute-start = (bf16[128,640]{1,0:T(8,128)(2,1)}, bf16[128,640]{1,0:T(8,128)(2,1)}, u32[]{:S(2)}, u32[]{:S(2)}) collective-permute-start(bf16[128,640]{1,0:T(8,128)(2,1)} %param.21), channel_id=1, source_target_pairs={{0,4},{4,8},{8,12},{12,16},{16,20},{20,24},{24,28},{28,0},{1,5},{5... | collective-permute-start | bytes 491528 | tf_op jit(solution)/shard_map/ppermute | solution.py:88
  59.9 56.4 %collective-permute-start.1 = (bf16[128,640]{1,0:T(8,128)(2,1)}, bf16[128,640]{1,0:T(8,128)(2,1)}, u32[]{:S(2)}, u32[]{:S(2)}) collective-permute-start(bf16[128,640]{1,0:T(8,128)(2,1)} %param.21), channel_id=1, source_target_pairs={{0,8},{4,12},{8,16},{12,20},{16,24},{20,28},{24,0},{28,4},{1,9},{5... | collective-permute-start | bytes 491528 | tf_op jit(solution)/shard_map/ppermute | solution.py:88
  61.4 57.1 %collective-permute-start.2 = (bf16[128,640]{1,0:T(8,128)(2,1)}, bf16[128,640]{1,0:T(8,128)(2,1)}, u32[]{:S(2)}, u32[]{:S(2)}) collective-permute-start(bf16[128,640]{1,0:T(8,128)(2,1)} %param.21), channel_id=1, source_target_pairs={{0,12},{4,16},{8,20},{12,24},{16,28},{20,0},{24,4},{28,8},{1,13},{... | collective-permute-start | bytes 491528 | tf_op jit(solution)/shard_map/ppermute | solution.py:88
  62.2 57.3 %collective-permute-start.3 = (bf16[128,640]{1,0:T(8,128)(2,1)}, bf16[128,640]{1,0:T(8,128)(2,1)}, u32[]{:S(2)}, u32[]{:S(2)}) collective-permute-start(bf16[128,640]{1,0:T(8,128)(2,1)} %param.21), channel_id=1, source_target_pairs={{0,16},{4,20},{8,24},{12,28},{16,0},{20,4},{24,8},{28,12},{1,17},{... | collective-permute-start | bytes 491528 | tf_op jit(solution)/shard_map/ppermute | solution.py:88
  65.0 55.4 %collective-permute-start.4 = (bf16[128,640]{1,0:T(8,128)(2,1)}, bf16[128,640]{1,0:T(8,128)(2,1)}, u32[]{:S(2)}, u32[]{:S(2)}) collective-permute-start(bf16[128,640]{1,0:T(8,128)(2,1)} %param.21), channel_id=1, source_target_pairs={{0,20},{4,24},{8,28},{12,0},{16,4},{20,8},{24,12},{28,16},{1,21},{... | collective-permute-start | bytes 491528 | tf_op jit(solution)/shard_map/ppermute | solution.py:88
  76.7 8.8 %copy-start.62 = (f32[1536]{0:T(1024)}, f32[1536]{0:T(1024)S(1)}, u32[]{:S(2)}) copy-start(f32[1536]{0:T(1024)S(1)} %multiply_reduce_fusion.14) | copy-start | bytes 18436
  92.2 16.3 %copy-start.22 = (bf16[1536,4,128]{2,0,1:T(8,128)(2,1)}, bf16[1536,4,128]{2,0,1:T(8,128)(2,1)S(1)}, u32[]{:S(2)}) copy-start(bf16[1536,4,128]{2,0,1:T(8,128)(2,1)S(1)} %get-tuple-element.136) | copy-start | bytes 4718596
  92.2 16.3 %copy-start.25 = (bf16[1536,4,128]{2,0,1:T(8,128)(2,1)}, bf16[1536,4,128]{2,0,1:T(8,128)(2,1)S(1)}, u32[]{:S(2)}) copy-start(bf16[1536,4,128]{2,0,1:T(8,128)(2,1)S(1)} %get-tuple-element.137) | copy-start | bytes 4718596
  111.9 19.0 %copy-start.30 = (bf16[1536,4,256]{0,2,1:T(8,128)(2,1)}, bf16[1536,4,256]{0,2,1:T(8,128)(2,1)S(1)}, u32[]{:S(2)}) copy-start(bf16[1536,4,256]{0,2,1:T(8,128)(2,1)S(1)} %pad_maximum_fusion.2) | copy-start | bytes 9437188
  113.2 15.1 %collective-permute-start.5 = (bf16[128,640]{1,0:T(8,128)(2,1)}, bf16[128,640]{1,0:T(8,128)(2,1)S(1)}, u32[]{:S(2)}, u32[]{:S(2)}) collective-permute-start(bf16[128,640]{1,0:T(8,128)(2,1)} %param.21), channel_id=1, source_target_pairs={{0,24},{4,28},{8,0},{12,4},{16,8},{20,12},{24,16},{28,20},{1,25},{... | collective-permute-start | bytes 491528 | tf_op jit(solution)/shard_map/ppermute | solution.py:88
  116.3 12.3 %collective-permute-start.6 = (bf16[128,640]{1,0:T(8,128)(2,1)}, bf16[128,640]{1,0:T(8,128)(2,1)S(1)}, u32[]{:S(2)}, u32[]{:S(2)}) collective-permute-start(bf16[128,640]{1,0:T(8,128)(2,1)} %param.21), channel_id=1, source_target_pairs={{0,28},{4,0},{8,4},{12,8},{16,12},{20,16},{24,20},{28,24},{1,29},{... | collective-permute-start | bytes 491528 | tf_op jit(solution)/shard_map/ppermute | solution.py:88
  135.2 10.4 %copy-start.32 = (bf16[1536,640]{0,1:T(8,128)(2,1)}, bf16[1536,640]{0,1:T(8,128)(2,1)S(1)}, u32[]{:S(2)}) copy-start(bf16[1536,640]{0,1:T(8,128)(2,1)S(1)} %multiply_convert_fusion.2) | copy-start | bytes 5898244
  175.6 7.5 %copy-start.11 = (bf16[1536,640]{0,1:T(8,128)(2,1)S(1)}, bf16[1536,640]{0,1:T(8,128)(2,1)}, u32[]{:S(2)}) copy-start(bf16[1536,640]{0,1:T(8,128)(2,1)} %copy.145) | copy-start | bytes 5898244
  175.6 7.5 %copy-start.68 = (f32[640]{0:T(1024)S(1)}, f32[640]{0:T(1024)}, u32[]{:S(2)}) copy-start(f32[640]{0:T(1024)} %get-tuple-element.110) | copy-start | bytes 7684
  175.6 7.5 %copy-start.77 = (pred[1536]{0:T(1024)(128)(4,1)S(1)}, pred[1536]{0:T(1024)(128)(4,1)}, u32[]{:S(2)}) copy-start(pred[1536]{0:T(1024)(128)(4,1)} %iota_compare_fusion.2) | copy-start | bytes 4612
  195.8 172.5 %reduce-scatter.8.cloned.1.call-start = ((), (), s32[]{:S(2)}) async-start(), calls=%async_computation.10 | async-start | bytes 2949120 | tf_op jit(solution)/shard_map/reduce_scatter | solution.py:61
  229.6 9.4 %copy-start.74 = (f32[4,512]{1,0:T(4,128)S(1)}, f32[4,512]{1,0:T(4,128)}, u32[]{:S(2)}) copy-start(f32[4,512]{1,0:T(4,128)} %copy-done.73) | copy-start | bytes 24580
  229.6 9.4 %copy-start.76 = (f32[4,512]{1,0:T(4,128)S(1)}, f32[4,512]{1,0:T(4,128)}, u32[]{:S(2)}) copy-start(f32[4,512]{1,0:T(4,128)} %copy-done.75) | copy-start | bytes 24580
  229.6 9.5 %copy-start.70 = (f32[4,512]{1,0:T(4,128)S(1)}, f32[4,512]{1,0:T(4,128)}, u32[]{:S(2)}) copy-start(f32[4,512]{1,0:T(4,128)} %copy-done.69) | copy-start | bytes 24580
  229.6 9.5 %copy-start.72 = (f32[4,512]{1,0:T(4,128)S(1)}, f32[4,512]{1,0:T(4,128)}, u32[]{:S(2)}) copy-start(f32[4,512]{1,0:T(4,128)} %copy-done.71) | copy-start | bytes 24580
  238.9 129.4 %reduce-scatter.10.cloned.1.call-start = ((), (), s32[]{:S(2)}) async-start(), calls=%async_computation.11 | async-start | bytes 2949120 | tf_op jit(solution)/shard_map/reduce_scatter | solution.py:61
  239.7 169.6 %reduce-scatter.12.cloned.1.call-start = ((), (), s32[]{:S(2)}) async-start(), calls=%async_computation.12 | async-start | bytes 1474560 | tf_op jit(solution)/shard_map/reduce_scatter | solution.py:61
  239.7 7.6 %copy-start.7 = (f32[1536,640]{0,1:T(8,128)S(1)}, f32[1536,640]{0,1:T(8,128)}, u32[]{:S(2)}) copy-start(f32[1536,640]{0,1:T(8,128)} %copy-done.5) | copy-start | bytes 11796484
  239.8 7.6 %copy-start.83 = (bf16[640,2048]{1,0:T(8,128)(2,1)S(1)}, bf16[640,2048]{1,0:T(8,128)(2,1)}, u32[]{:S(2)}) copy-start(bf16[640,2048]{1,0:T(8,128)(2,1)} %all-gather.9.cloned.1.call-done) | copy-start | bytes 7864324
  247.4 7.4 %copy-start.10 = (f32[1536,640]{0,1:T(8,128)S(1)}, f32[1536,640]{0,1:T(8,128)}, u32[]{:S(2)}) copy-start(f32[1536,640]{0,1:T(8,128)} %copy-done.9) | copy-start | bytes 11796484
  270.8 172.7 %reduce-scatter.14.cloned.1.call-start = ((), (), s32[]{:S(2)}) async-start(), calls=%async_computation.13 | async-start | bytes 2396160 | tf_op jit(solution)/shard_map/reduce_scatter | solution.py:61
  274.5 20.7 %copy-start.12 = (bf16[1536,4,256]{2,0,1:T(8,128)(2,1)}, bf16[1536,4,256]{2,0,1:T(8,128)(2,1)S(1)}, u32[]{:S(2)}) copy-start(bf16[1536,4,256]{2,0,1:T(8,128)(2,1)S(1)} %copy.148) | copy-start | bytes 9437188
  281.4 7.6 %copy-start.2 = (f32[4,512,512]{1,2,0:T(8,128)S(1)}, f32[4,512,512]{1,2,0:T(8,128)}, u32[]{:S(2)}) copy-start(f32[4,512,512]{1,2,0:T(8,128)} %copy-done.1) | copy-start | bytes 12582916
  281.4 13.8 %slice-start = ((s8[12582912]{0:T(1024)(128)(4,1)}), s8[4194304]{0:T(1024)(128)(4,1)S(1)}, s32[]{:S(2)}) async-start(s8[12582912]{0:T(1024)(128)(4,1)} %bitcast.161), calls=%async_computation.14 | async-start | bytes 8388608
  281.4 13.8 %slice-start.1 = ((s8[12582912]{0:T(1024)(128)(4,1)}), s8[4194304]{0:T(1024)(128)(4,1)S(1)}, s32[]{:S(2)}) async-start(s8[12582912]{0:T(1024)(128)(4,1)} %bitcast.161), calls=%async_computation.15 | async-start | bytes 8388608
  293.8 62.8 %collective-permute-start.7 = (bf16[256,640]{1,0:T(8,128)(2,1)}, bf16[256,640]{1,0:T(8,128)(2,1)}, u32[]{:S(2)}, u32[]{:S(2)}) collective-permute-start(bf16[256,640]{1,0:T(8,128)(2,1)} %reduce-scatter.6.cloned.1.call-done), channel_id=1, source_target_pairs={{0,1},{1,0},{2,3},{3,2},{4,5},{5,4},{6,7},{7,6},{8,9},{9,8},{10,11... | collective-permute-start | bytes 983048 | tf_op jit(solution)/shard_map/ppermute | solution.py:74
  301.4 13.2 %slice-start.7 = ((s8[8388608]{0:T(1024)(128)(4,1)}), s8[4194304]{0:T(1024)(128)(4,1)S(1)}, s32[]{:S(2)}) async-start(s8[8388608]{0:T(1024)(128)(4,1)} %bitcast.167), calls=%async_computation.21 | async-start | bytes 8388608
  301.4 7.9 %copy-start.36 = (bf16[1536,128]{0,1:T(8,128)(2,1)S(1)}, bf16[1536,128]{0,1:T(8,128)(2,1)}, u32[]{:S(2)}) copy-start(bf16[1536,128]{0,1:T(8,128)(2,1)} %get-tuple-element.146) | copy-start | bytes 1179652
  301.4 13.2 %slice-start.8 = ((s8[8388608]{0:T(1024)(128)(4,1)}), s8[4194304]{0:T(1024)(128)(4,1)S(1)}, s32[]{:S(2)}) async-start(s8[8388608]{0:T(1024)(128)(4,1)} %bitcast.167), calls=%async_computation.22 | async-start | bytes 8388608
  327.2 9.7 %slice-start.3 = ((s8[6291456]{0:T(1024)(128)(4,1)}), s8[4194304]{0:T(1024)(128)(4,1)S(1)}, s32[]{:S(2)}) async-start(s8[6291456]{0:T(1024)(128)(4,1)} %bitcast.163), calls=%async_computation.17 | async-start | bytes 8388608
  357.8 10.6 %copy-start.59 = (f32[1536]{0:T(1024)S(1)}, f32[1536]{0:T(1024)}, u32[]{:S(2)}) copy-start(f32[1536]{0:T(1024)} %copy-done.58) | copy-start | bytes 18436
  357.8 10.6 %copy-start.82 = (f32[128]{0:T(128)S(1)}, f32[128]{0:T(128)}, u32[]{:S(2)}) copy-start(f32[128]{0:T(128)} %negate_power_fusion) | copy-start | bytes 1540
  357.8 9.7 %collective-permute-start.8 = (bf16[256,640]{1,0:T(8,128)(2,1)S(1)}, bf16[256,640]{1,0:T(8,128)(2,1)S(1)}, u32[]{:S(2)}, u32[]{:S(2)}) collective-permute-start(bf16[256,640]{1,0:T(8,128)(2,1)S(1)} %add_convert_fusion.4), channel_id=1, source_target_pairs={{0,2},{1,3},{2,0},{3,1},{4,6},{5,7},{6,4},{7,5},{8,10},{9,11},{10,... | collective-permute-start | bytes 983048 | tf_op jit(solution)/shard_map/ppermute | solution.py:74
  364.0 7.5 %copy-start.56 = (f32[1536]{0:T(1024)S(1)}, f32[1536]{0:T(1024)}, u32[]{:S(2)}) copy-start(f32[1536]{0:T(1024)} %copy-done.55) | copy-start | bytes 18436
  364.0 7.5 %copy-start.78 = (f32[256]{0:T(256)S(1)}, f32[256]{0:T(256)}, u32[]{:S(2)}) copy-start(f32[256]{0:T(256)} %reshape.464) | copy-start | bytes 3076
  364.0 9.6 %copy-start.63 = (f32[1536]{0:T(1024)S(1)}, f32[1536]{0:T(1024)}, u32[]{:S(2)}) copy-start(f32[1536]{0:T(1024)} %copy-done.62) | copy-start | bytes 18436
  375.4 16.1 %collective-permute-start.9 = (bf16[80,2048]{1,0:T(8,128)(2,1)}, bf16[80,2048]{1,0:T(8,128)(2,1)}, u32[]{:S(2)}, u32[]{:S(2)}) collective-permute-start(bf16[80,2048]{1,0:T(8,128)(2,1)} %reduce-scatter.8.cloned.1.call-done), channel_id=1, source_target_pairs={{0,2},{1,3},{2,0},{3,1},{4,6},{5,7},{6,4},{7,5},{8,10},{9,11},{10,... | collective-permute-start | bytes 983048 | tf_op jit(solution)/shard_map/ppermute | solution.py:74
  390.5 10.7 %collective-permute-start.11 = (bf16[80,2048]{1,0:T(8,128)(2,1)S(1)}, bf16[80,2048]{1,0:T(8,128)(2,1)S(1)}, u32[]{:S(2)}, u32[]{:S(2)}) collective-permute-start(bf16[80,2048]{1,0:T(8,128)(2,1)S(1)} %copy-done.50), channel_id=1, source_target_pairs={{0,1},{1,0},{2,3},{3,2},{4,5},{5,4},{6,7},{7,6},{8,9},{9,8},{10,11... | collective-permute-start | bytes 983048 | tf_op jit(solution)/shard_map/ppermute | solution.py:74
  392.6 13.3 %collective-permute-start.10 = (bf16[80,2048]{1,0:T(8,128)(2,1)S(1)}, bf16[80,2048]{1,0:T(8,128)(2,1)S(1)}, u32[]{:S(2)}, u32[]{:S(2)}) collective-permute-start(bf16[80,2048]{1,0:T(8,128)(2,1)S(1)} %add_convert_fusion.3), channel_id=1, source_target_pairs={{0,1},{1,0},{2,3},{3,2},{4,5},{5,4},{6,7},{7,6},{8,9},{9,8},{10,11... | collective-permute-start | bytes 983048 | tf_op jit(solution)/shard_map/ppermute | solution.py:74
  401.2 7.1 %collective-permute-start.12 = (bf16[80,2048]{1,0:T(8,128)(2,1)S(1)}, bf16[80,2048]{1,0:T(8,128)(2,1)S(1)}, u32[]{:S(2)}, u32[]{:S(2)}) collective-permute-start(bf16[80,2048]{1,0:T(8,128)(2,1)S(1)} %add_convert_fusion.2), channel_id=1, source_target_pairs={{0,2},{1,3},{2,0},{3,1},{4,6},{5,7},{6,4},{7,5},{8,10},{9,11},{10,... | collective-permute-start | bytes 983048 | tf_op jit(solution)/shard_map/ppermute | solution.py:74
  413.5 8.2 %copy-start.54 = (bf16[128,640]{1,0:T(8,128)(2,1)S(1)}, bf16[128,640]{1,0:T(8,128)(2,1)}, u32[]{:S(2)}) copy-start(bf16[128,640]{1,0:T(8,128)(2,1)} %reduce-scatter.12.cloned.1.call-done) | copy-start | bytes 491524
  413.5 31.4 %copy-start.61 = (f32[1536]{0:T(1024)S(1)}, f32[1536]{0:T(1024)}, u32[]{:S(2)}) copy-start(f32[1536]{0:T(1024)} %copy-done.60) | copy-start | bytes 18436
  421.7 23.2 %collective-permute-start.15 = (bf16[128,640]{1,0:T(8,128)(2,1)S(1)}, bf16[128,640]{1,0:T(8,128)(2,1)S(1)}, u32[]{:S(2)}, u32[]{:S(2)}) collective-permute-start(bf16[128,640]{1,0:T(8,128)(2,1)S(1)} %copy-done.54), channel_id=1, source_target_pairs={{0,2},{1,3},{2,0},{3,1},{4,6},{5,7},{6,4},{7,5},{8,10},{9,11},{10,... | collective-permute-start | bytes 491528 | tf_op jit(solution)/shard_map/ppermute | solution.py:74
  443.5 7.5 %collective-permute-start.13 = (bf16[80,1664]{1,0:T(8,128)(2,1)}, bf16[80,1664]{1,0:T(8,128)(2,1)S(1)}, u32[]{:S(2)}, u32[]{:S(2)}) collective-permute-start(bf16[80,1664]{1,0:T(8,128)(2,1)} %reduce-scatter.14.cloned.1.call-done), channel_id=1, source_target_pairs={{0,1},{1,0},{2,3},{3,2},{4,5},{5,4},{6,7},{7,6},{8,9},{9,8},{10,11... | collective-permute-start | bytes 798728 | tf_op jit(solution)/shard_map/ppermute | solution.py:74
  445.0 20.2 %collective-permute-start.16 = (bf16[128,640]{1,0:T(8,128)(2,1)S(1)}, bf16[128,640]{1,0:T(8,128)(2,1)S(1)}, u32[]{:S(2)}, u32[]{:S(2)}) collective-permute-start(bf16[128,640]{1,0:T(8,128)(2,1)S(1)} %add_convert_fusion.6), channel_id=1, source_target_pairs={{0,1},{1,0},{2,3},{3,2},{4,5},{5,4},{6,7},{7,6},{8,9},{9,8},{10,11... | collective-permute-start | bytes 491528 | tf_op jit(solution)/shard_map/ppermute | solution.py:74
  452.0 14.0 %collective-permute-start.14 = (bf16[80,1664]{1,0:T(8,128)(2,1)S(1)}, bf16[80,1664]{1,0:T(8,128)(2,1)S(1)}, u32[]{:S(2)}, u32[]{:S(2)}) collective-permute-start(bf16[80,1664]{1,0:T(8,128)(2,1)S(1)} %add_convert_fusion.5), channel_id=1, source_target_pairs={{0,2},{1,3},{2,0},{3,1},{4,6},{5,7},{6,4},{7,5},{8,10},{9,11},{10,... | collective-permute-start | bytes 798728 | tf_op jit(solution)/shard_map/ppermute | solution.py:74
  459.7 7.2 %copy-start.49 = (bf16[80,512]{1,0:T(8,128)(2,1)S(1)}, bf16[80,512]{1,0:T(8,128)(2,1)}, u32[]{:S(2)}) copy-start(bf16[80,512]{1,0:T(8,128)(2,1)} %param.20) | copy-start | bytes 245764
  459.7 9.5 %copy-start.81 = (bf16[80]{0:T(256)(128)(2,1)S(1)}, bf16[80]{0:T(256)(128)(2,1)}, u32[]{:S(2)}) copy-start(bf16[80]{0:T(256)(128)(2,1)} %param.25) | copy-start | bytes 484
  (59 other events, 219.2 us)
Sparse Core Ops, SparseCore 0:
  13.8 32.0 all-gather.4
  47.5 54.6 all-gather.6
  103.9 37.2 all-gather.8
  142.7 32.8 all-gather.10
  196.0 36.3 reduce-scatter.5
  239.1 36.3 reduce-scatter.7
  277.8 36.6 reduce-scatter.9
  316.7 32.2 reduce-scatter.11
  409.4 34.0 reduce-scatter.13

commit v2 on v1

--- a/solution.py
+++ b/solution.py
@@ -302,9 +302,7 @@
         [qkv_grad, grad_cols, jnp.zeros((d_model, 123), jnp.bfloat16)], axis=1
     )
     grad_pack, d_qkv_low = lax.optimization_barrier((grad_pack, d_qkv_low))
-    sum_gate, sum_upward, project_share, grad_pack = lax.optimization_barrier(
-        (sum_gate, sum_upward, project_share, grad_pack)
-    )
+    project_share, grad_pack = lax.optimization_barrier((project_share, grad_pack))
     pack_share = scatter(grad_pack)
     d_h = right_dot(d_qkv_low, qkv_full)
     d_input_part = back_input(d_h)[0]

time: 484 us -> 467 us (0.965)
  waiting for transfers between devices: 79.4 us -> 57.5 us
  local copies, waits for them, and re-layouts: 74.6 us -> 79.6 us
    reduce_scatter x5, waiting for transfers between devices: 21.1 us -> 1.02 us  [scatter(): return lax.psum_scatter(grad, 'shard', scatter_dimension=0, tiled=True)]
    unnamed x198 -> x200, local copies, waits for them, and re-layouts: 29.4 us -> 29 us
  transfers between devices with their start and end apart: 26 -> 26, of which waited for: 10 -> 10; matrix products, arithmetic and copies ran while one was open for 67% -> 70% of each run, Pallas kernels for 0% -> 0%
where the time goes in v2:
time: 467 us; the launch traced here: 460 us
  matrix products  195 us (42%)
  other arithmetic  89.5 us (19%)
  local copies, waits for them, and re-layouts  79.6 us (17%)
  waiting for transfers between devices  57.5 us (12%)
  starting transfers between devices  22.1 us (5%)
  between operations  15.7 us (3%)
    dot_general x5, matrix products, right_dot(): lax.dot_general(left, right, (((1,), (1,)), ((), ())), preferred_element_...  49.4 us
    dot_general x5, matrix products, left_dot(): lax.dot_general(left, right, (((0,), (0,)), ((), ())), preferred_element_...  35.1 us
    unnamed x200, local copies, waits for them, and re-layouts  29 us
    ppermute x10, waiting for transfers between devices, rep_sum(): other = lax.ppermute(total.astype(jnp.bfloat16), 'rep', pairs)  20.5 us
    dot_general x1, matrix products, shards(): upper = jnp.dot(h_two_low, upward_full, preferred_element_type=jnp.float32)  16.8 us
    dot_general x3, matrix products, shards(): jnp.einsum('qhd,kd->hqk', d_block, v_low[:seen], preferred_element_type=j...  16.8 us
    convert_element_type x3, other arithmetic, shards(): d_logits = (probs * (d_probs - spread)).astype(jnp.bfloat16)  13.8 us
    all_gather x1, waiting for transfers between devices, shards(): lax.all_gather(jnp.concatenate([w_query, w_keyval, gain_cols], axis=1), '...  13.7 us
  transfers between devices with their start and end apart: 26, of which 10 were waited for; matrix products, arithmetic and copies ran while one was open for 70% of the time, Pallas kernels for 0%

profile of v2, /device:TPU:0, one launch (start us, length us, event | category | flops | bytes accessed | tf_op | source)
XLA Modules:
  0.0 459.7 jit_solution(16941350317220493514)
XLA Ops:
  19.5 2.7 copy.128
  22.7 4.3 copy.145
  32.2 13.7 %all-gather.5.cloned.1.call-done = bf16[640,1664]{1,0:T(8,128)(2,1)} async-done(((bf16[80,1664]{1,0:T(8,128)(2,1)}), bf16[640,1664]{1,0:T(8,128)(2,1)}) %all-gather.5.cloned.1.call-update) | async-done | bytes 2129936 | tf_op jit(solution)/shard_map/all_gather | solution.py:130
  48.7 6.8 %multiply_reduce_fusion.2 = (f32[1536,4]{0,1:T(4,128)}, f32[1536,1024]{0,1:T(8,128)}) fusion(bf16[640,1664]{1,0:T(8,128)(2,1)} %all-gather.5.cloned.1.call-done, bf16[1536,640]{0,1:T(8,128)(2,1)S(1)} %copy.128, f32[640]{0:T(1024)S(1)} %get-tuple-element.109, f32[1536]{0:T(1024)S(1)} %fusion.115), kind=kOutput, calls=%fused_computation.47 | convolution fusion | flops 2020337664 | bytes 9601536 | tf_op jit(solution)/shard_map/dot_general | solution.py:151
  55.5 4.3 fusion.139
  62.3 2.8 collective-permute-start.3
  65.3 6.6 %copy.136 = f32[1536,4,256]{2,0,1:T(8,128)} copy(f32[1536,4,256]{0,2,1:T(8,128)} %bitcast.171) | data formatting | bytes 12582912 | tf_op jit(solution)/shard_map/reshape | solution.py:151
  78.6 4.8 %multiply_cosine_fusion = (f32[1536,128]{0,1:T(8,128)}, f32[1536,128]{0,1:T(8,128)}, bf16[1536,128]{0,1:T(8,128)(2,1)}, bf16[1536,128]{0,1:T(8,128)(2,1)}) fusion(f32[128]{0:T(128)} %negate_power_fusion, f32[1536]{0:T(1024)S(1)} %subtract_convert_fusion.1, f32[1536,256]{0,1:T(8,128)S(1)} %multiply_multiply_fusion.4), kind=kLoop, calls=%fused_computation.145 | loop fusion | flops 1769472 | bytes 3938816 | tf_op jit(solution)/shard_map/cos | solution.py:22
  83.4 2.3 copy.138
  85.7 2.3 copy.137
  88.0 3.5 multiply_multiply_fusion.3
  92.9 2.7 fusion.138
  95.7 4.6 %fusion.140 = (f32[4,512]{1,0:T(4,128)S(1)}, f32[4,512,1024]{1,2,0:T(8,128)}) fusion(bf16[1536,4,128]{2,0,1:T(8,128)(2,1)S(1)} %get-tuple-element.132, bf16[1536,4,128]{2,0,1:T(8,128)(2,1)S(1)} %get-tuple-element.133, bf16[1536,128]{0,1:T(8,128)(2,1)S(1)} %copy-done.40, bf16[1536,128]{0,1:T(8,128)(2,1)S(1)} %copy-done.37, pred[512,1024]{0,1:T(8,128)(4,1)S(1)} %copy-done.48), kind=kOutput, calls=%fused_computation.272 | convolution fusion | flops 1083176960 | bytes 12853248 | tf_op jit(solution)/shard_map/qhd,kd->hqk/dot_general | solution.py:173
  102.7 3.0 fusion.68
  113.4 2.3 collective-permute-start.5
  121.8 6.3 %collective-permute-done.5 = bf16[128,640]{1,0:T(8,128)(2,1)S(1)} collective-permute-done((bf16[128,640]{1,0:T(8,128)(2,1)}, bf16[128,640]{1,0:T(8,128)(2,1)S(1)}, u32[]{:S(2)}, u32[]{:S(2)}) %collective-permute-start.5) | collective-permute-done | bytes 163872 | tf_op jit(solution)/shard_map/ppermute | solution.py:88
  128.9 2.4 multiply_reduce_fusion.11
  135.6 10.4 %fusion.142 = f32[1536,2048]{1,0:T(8,128)} fusion(bf16[1536,640]{0,1:T(8,128)(2,1)S(1)} %multiply_convert_fusion.2, bf16[640,2048]{1,0:T(8,128)(2,1)} %all-gather.7.cloned.1.call-done), kind=kOutput, calls=%fused_computation.274 | convolution fusion | flops 4026531840 | bytes 17170432 | tf_op jit(solution)/shard_map/dot_general | solution.py:204
  146.0 16.8 %multiply_convert_fusion.1 = (bf16[1536,2048]{1,0:T(8,128)(2,1)}, f32[1536,2048]{1,0:T(8,128)}) fusion(f32[1536,2048]{1,0:T(8,128)} %fusion.142, bf16[1536,640]{0,1:T(8,128)(2,1)S(1)} %multiply_convert_fusion.2, bf16[640,2048]{1,0:T(8,128)(2,1)} %all-gather.9.cloned.1.call-done), kind=kOutput, calls=%fused_computation.17 | convolution fusion | flops 4057989120 | bytes 36044800 | tf_op jit(solution)/shard_map/dot_general | solution.py:205
  162.9 12.7 %all-gather.11.cloned.1.call-done = bf16[2048,640]{1,0:T(8,128)(2,1)} async-done(((bf16[256,640]{1,0:T(8,128)(2,1)}), bf16[2048,640]{1,0:T(8,128)(2,1)}) %all-gather.11.cloned.1.call-update) | async-done | bytes 2621456 | tf_op jit(solution)/shard_map/all_gather | solution.py:147
  175.6 7.5 %multiply_reduce_fusion.9 = (f32[1536]{0:T(1024)S(1)}, f32[1536,640]{0,1:T(8,128)S(1)}) fusion(bf16[1536,2048]{1,0:T(8,128)(2,1)} %get-tuple-element.159, bf16[2048,640]{1,0:T(8,128)(2,1)} %all-gather.11.cloned.1.call-done), kind=kOutput, calls=%fused_computation.84 | convolution fusion | flops 4028496384 | bytes 12851200 | tf_op jit(solution)/shard_map/dot_general | solution.py:210
  185.1 2.8 fusion.29
  189.2 6.6 %convolution_convert_fusion.3 = bf16[2048,640]{1,0:T(8,128)(2,1)} fusion(bf16[1536,2048]{1,0:T(8,128)(2,1)S(1)} %bitcast.180, bf16[1536,640]{0,1:T(8,128)(2,1)S(1)} %get-tuple-element.36), kind=kOutput, calls=%fused_computation.98 | convolution fusion | flops 4027842560 | bytes 10878976 | tf_op jit(solution)/shard_map/dot_general | solution.py:49
  195.9 24.5 %multiply_convert_fusion = (bf16[1536,2048]{1,0:T(8,128)(2,1)}, bf16[1536,2048]{1,0:T(8,128)(2,1)}) fusion(f32[1536,2048]{1,0:T(8,128)} %fusion.142, f32[1536,2048]{1,0:T(8,128)} %get-tuple-element.160, bf16[1536,640]{0,1:T(8,128)(2,1)} %copy-done.36, bf16[2048,640]{1,0:T(8,128)(2,1)} %all-gather.11.cloned.1.call-done), kind=kOutput, calls=%fused_computation.16 | convolution fusion | flops 4102029312 | bytes 42336256 | tf_op jit(solution)/shard_map/dot_general | solution.py:55
  220.4 9.2 %convolution_convert_fusion.2 = bf16[640,2048]{1,0:T(8,128)(2,1)} fusion(bf16[1536,640]{0,1:T(8,128)(2,1)} %copy-done.35, bf16[1536,2048]{1,0:T(8,128)(2,1)} %get-tuple-element.37), kind=kOutput, calls=%fused_computation.97 | convolution fusion | flops 4027842560 | bytes 10878976 | tf_op jit(solution)/shard_map/dot_general | solution.py:49
  229.6 9.3 %convolution_convert_fusion.1 = bf16[640,2048]{1,0:T(8,128)(2,1)} fusion(bf16[1536,640]{0,1:T(8,128)(2,1)} %copy-done.35, bf16[1536,2048]{1,0:T(8,128)(2,1)} %get-tuple-element.38), kind=kOutput, calls=%fused_computation.96 | convolution fusion | flops 4027842560 | bytes 10878976 | tf_op jit(solution)/shard_map/dot_general | solution.py:49
  239.8 7.9 %fusion.143 = f32[1536,640]{0,1:T(8,128)S(1)} fusion(bf16[1536,2048]{1,0:T(8,128)(2,1)} %get-tuple-element.37, bf16[640,2048]{1,0:T(8,128)(2,1)} %all-gather.7.cloned.1.call-done), kind=kOutput, calls=%fused_computation.275 | convolution fusion | flops 4026531840 | bytes 12845056 | tf_op jit(solution)/shard_map/dot_general | solution.py:55
  247.7 7.3 %multiply_reduce_fusion.4 = (bf16[640]{0:T(1024)(128)(2,1)S(1)}, f32[1536]{0:T(1024)S(1)}, f32[1536,640]{0,1:T(8,128)S(1)}) fusion(f32[1536,640]{0,1:T(8,128)S(1)} %copy-done.7, f32[1536]{0:T(1024)S(1)} %fusion.118, f32[640]{0:T(1024)S(1)} %copy-done.70, f32[1536,640]{0,1:T(8,128)S(1)} %fusion.143, bf16[1536,2048]{1,0:T(8,128)(2,1)} %get-tuple-element.38, ...), kind=kOutput, calls=%fused_computation.76 | convolution fusion | flops 4033411072 | bytes 20725504 | tf_op jit(solution)/shard_map/dot_general | solution.py:55
  255.1 2.4 multiply_reduce_fusion.5
  260.8 3.8 convolution_convert_fusion.5
  267.0 4.0 convolution_convert_fusion
  271.1 3.4 copy.148
  274.5 6.9 %fusion.64 = f32[1024,256]{0,1:T(8,128)} fusion(f32[4,512,1024]{1,2,0:T(8,128)} %get-tuple-element.154, f32[4,512]{1,0:T(4,128)S(1)} %log_add_fusion.1, bf16[1536,4,256]{2,0,1:T(8,128)(2,1)S(1)} %copy.148), kind=kOutput, calls=%fused_computation.135 | convolution fusion | flops 1077936128 | bytes 10493952 | tf_op jit(solution)/shard_map/hqk,qhd->kd/dot_general | solution.py:266
  281.4 7.6 %fusion.12 = (f32[4,512]{1,0:T(4,128)S(1)}, f32[1024,512,4]{1,0,2:T(8,128)}) fusion(f32[4,512,1024]{1,2,0:T(8,128)} %get-tuple-element.154, f32[4,512]{1,0:T(4,128)S(1)} %log_add_fusion.1, bf16[1536,4,256]{2,0,1:T(8,128)(2,1)S(1)} %copy.148, bf16[1536,512]{0,1:T(8,128)(2,1)S(1)} %copy-done.19), kind=kOutput, calls=%fused_computation.26 | convolution fusion | flops 1080031232 | bytes 18366464 | tf_op jit(solution)/shard_map/qhd,kd->hqk/dot_general | solution.py:248
  290.8 3.0 fusion.24
  295.2 6.2 %fusion.7 = (f32[4,512]{1,0:T(4,128)S(1)}, f32[1536,512,4]{1,0,2:T(8,128)}) fusion(f32[4,512,1536]{1,2,0:T(8,128)S(1)} %bitcast.162, f32[4,512]{1,0:T(4,128)S(1)} %log_add_fusion, bf16[1536,4,256]{2,0,1:T(8,128)(2,1)S(1)} %copy.148, bf16[1536,512]{0,1:T(8,128)(2,1)S(1)} %copy-done.19), kind=kOutput, calls=%fused_computation.11 | convolution fusion | flops 1620047872 | bytes 27017216 | tf_op jit(solution)/shard_map/qhd,kd->hqk/dot_general | solution.py:248
  301.4 7.9 %fusion.9 = bf16[4,512,1536]{1,2,0:T(8,128)(2,1)S(1)} fusion(f32[1536,512,4]{1,0,2:T(8,128)} %get-tuple-element.165, f32[4,512,1536]{1,2,0:T(8,128)S(1)} %bitcast.162, f32[4,512]{1,0:T(4,128)S(1)} %get-tuple-element.164, f32[4,512]{1,0:T(4,128)S(1)} %log_add_fusion), kind=kLoop, calls=%fused_computation.13 | loop fusion | flops 12582912 | bytes 31473664 | tf_op jit(solution)/shard_map/convert_element_type | solution.py:252
  309.3 5.2 %multiply_bitcast_fusion = f32[512,4,256]{2,0,1:T(8,128)} fusion(bf16[4,512,1536]{1,2,0:T(8,128)(2,1)S(1)} %fusion.9, bf16[1536,128]{0,1:T(8,128)(2,1)S(1)} %copy-done.39, bf16[1536,128]{0,1:T(8,128)(2,1)} %get-tuple-element.143), kind=kOutput, calls=%fused_computation.115 | convolution fusion | flops 1612709888 | bytes 9175040 | tf_op jit(solution)/shard_map/hqk,kd->qhd/dot_general | solution.py:254
  314.6 4.7 %fusion.14 = bf16[4,512,1024]{1,2,0:T(8,128)(2,1)S(1)} fusion(f32[1024,512,4]{1,0,2:T(8,128)} %get-tuple-element.167, f32[4,512,1024]{1,2,0:T(8,128)S(1)} %bitcast.168, f32[4,512]{1,0:T(4,128)S(1)} %get-tuple-element.166, f32[4,512]{1,0:T(4,128)S(1)} %log_add_fusion.1), kind=kLoop, calls=%fused_computation.28 | loop fusion | flops 8388608 | bytes 20987904 | tf_op jit(solution)/shard_map/convert_element_type | solution.py:252
  319.3 3.1 multiply_bitcast_fusion.1
  327.2 5.5 %pad_maximum_fusion = f32[1536,4,256]{2,0,1:T(8,128)} fusion(f32[512,4,256]{2,0,1:T(8,128)} %multiply_bitcast_fusion, f32[512,4,256]{2,0,1:T(8,128)} %multiply_bitcast_fusion.1, f32[512,4,256]{2,0,1:T(8,128)S(1)} %multiply_bitcast_fusion.2), kind=kLoop, calls=%fused_computation.42 | loop fusion | flops 3145728 | bytes 12582912 | tf_op jit(solution)/shard_map/concatenate | solution.py:280
  332.8 4.2 multiply_add_fusion.1
  337.0 2.4 multiply_reduce_fusion
  339.5 3.9 fusion.17
  343.5 4.8 %fusion.49 = bf16[1536,256]{0,1:T(8,128)(2,1)} fusion(f32[4,512,1536]{1,2,0:T(8,128)S(1)} %bitcast.162, f32[4,512]{1,0:T(4,128)S(1)} %log_add_fusion, f32[1024,256]{0,1:T(8,128)S(1)} %copy-done.86, f32[512,256]{0,1:T(8,128)S(1)} %copy-done.49, bf16[1536,4,256]{2,0,1:T(8,128)(2,1)} %copy-done.13), kind=kOutput, calls=%fused_computation.112 | convolution fusion | flops 1618083840 | bytes 15998976 | tf_op jit(solution)/shard_map/hqk,qhd->kd/dot_general | solution.py:266
  348.3 2.3 fusion.67
  350.6 5.0 %copy.162 = bf16[1536,4,256]{0,2,1:T(8,128)(2,1)} copy(bf16[1536,4,256]{2,0,1:T(8,128)(2,1)} %fusion.17) | data formatting | bytes 6291456 | tf_op jit(solution)/shard_map/convert_element_type | solution.py:283
  356.5 2.1 fusion.74
  361.4 4.9 %fusion.45 = f32[1536,256]{0,1:T(8,128)S(1)} fusion(bf16[4,512,1536]{1,2,0:T(8,128)(2,1)} %copy-done.22, f32[1024,256]{0,1:T(8,128)} %fusion.67, f32[512,256]{0,1:T(8,128)S(1)} %fusion.74, bf16[1536,4,128]{2,0,1:T(8,128)(2,1)S(1)} %copy-done.28, bf16[1536,4,128]{2,0,1:T(8,128)(2,1)S(1)} %copy-done.25), kind=kOutput, calls=%fused_computation.110 | convolution fusion | flops 1613889536 | bytes 12582912 | tf_op jit(solution)/shard_map/hqk,qhd->kd/dot_general | solution.py:261
  366.3 3.1 collective-permute-done.8
  370.3 3.1 fusion.99
  373.5 2.5 multiply_reduce_fusion.12
  381.0 2.1 fusion.58
  383.1 6.2 %convolution_convert_fusion.4 = bf16[640,1536]{1,0:T(8,128)(2,1)} fusion(bf16[1536,640]{0,1:T(8,128)(2,1)S(1)} %copy-done.4, f32[640]{0:T(1024)S(1)} %copy-done.67, f32[1536]{0:T(1024)S(1)} %copy-done.56, bf16[1536,256]{0,1:T(8,128)(2,1)S(1)} %copy-done.44, bf16[1536,256]{0,1:T(8,128)(2,1)S(1)} %fusion.58, bf16[1536,1024]{0,1:T(8,128)(2,1)S(1)} %bitcast.170), kind=kOutput, calls=%fused_computation.99 | convolution fusion | flops 3038969856 | bytes 8659456 | tf_op jit(solution)/shard_map/dot_general | solution.py:49
  390.1 4.9 %concatenate.34 = bf16[640,1664]{1,0:T(8,128)(2,1)} concatenate(bf16[640,1536]{1,0:T(8,128)(2,1)} %convolution_convert_fusion.4, bf16[640,1]{1,0:T(8,128)(2,1)} %stack_reshape.10, bf16[640,1]{1,0:T(8,128)(2,1)} %stack_reshape.11, bf16[640,1]{1,0:T(8,128)(2,1)} %stack.17, bf16[640,1]{1,0:T(8,128)(2,1)} %stack.18, bf16[640,1]{1,0:T(8,128)(2,1)} %stack.19, ...), dimensions={1} | concatenate | bytes 4259840 | tf_op jit(solution)/shard_map/concatenate | solution.py:301
  395.0 3.8 pad_maximum_fusion.1
  398.8 4.1 copy.177
  405.0 5.7 %fusion.36 = (f32[1536]{0:T(1024)S(1)}, f32[1536,640]{0,1:T(8,128)S(1)}) fusion(bf16[1536,640]{0,1:T(8,128)(2,1)S(1)} %copy-done.4, f32[640]{0:T(1024)S(1)} %copy-done.68, bf16[1536,1536]{0,1:T(8,128)(2,1)} %pad_maximum_fusion.1, bf16[640,1664]{1,0:T(8,128)(2,1)} %all-gather.5.cloned.1.call-done), kind=kOutput, calls=%fused_computation.74 | convolution fusion | flops 3023829504 | bytes 12591616 | tf_op jit(solution)/shard_map/dot_general | solution.py:55
  411.7 3.2 fusion.32
  414.9 5.5 %copy.178 = f32[1536,640]{1,0:T(8,128)} copy(f32[1536,640]{0,1:T(8,128)} %fusion.32) | data formatting | bytes 7864320
  423.4 7.7 %collective-permute-done.15 = bf16[80,2048]{1,0:T(8,128)(2,1)S(1)} collective-permute-done((bf16[80,2048]{1,0:T(8,128)(2,1)S(1)}, bf16[80,2048]{1,0:T(8,128)(2,1)S(1)}, u32[]{:S(2)}, u32[]{:S(2)}) %collective-permute-start.15) | collective-permute-done | bytes 327712 | tf_op jit(solution)/shard_map/ppermute | solution.py:74
  435.1 2.6 collective-permute-done.14
  438.7 2.8 collective-permute-done.9
  444.9 4.2 collective-permute-done.10
  (357 shorter events, 99.1 us)
Async XLA Ops:
  7.2 38.7 %all-gather.5.cloned.1.call-start = ((), (), s32[]{:S(2)}) async-start(), calls=%async_computation.5 | async-start | bytes 2396160 | tf_op jit(solution)/shard_map/all_gather | solution.py:130
  13.7 121.9 %all-gather.7.cloned.1.call-start = ((), (), s32[]{:S(2)}) async-start(), calls=%async_computation.6 | async-start | bytes 2949120 | tf_op jit(solution)/shard_map/all_gather | solution.py:145
  14.4 131.6 %all-gather.9.cloned.1.call-start = ((), (), s32[]{:S(2)}) async-start(), calls=%async_computation.7 | async-start | bytes 2949120 | tf_op jit(solution)/shard_map/all_gather | solution.py:146
  15.2 160.4 %all-gather.11.cloned.1.call-start = ((), (), s32[]{:S(2)}) async-start(), calls=%async_computation.8 | async-start | bytes 2949120 | tf_op jit(solution)/shard_map/all_gather | solution.py:147
  15.7 255.4 %reduce-scatter.6.cloned.1.call-start = ((), (), s32[]{:S(2)}) async-start(), calls=%async_computation.9 | async-start | bytes 2949120 | tf_op jit(solution)/shard_map/reduce_scatter | solution.py:61
  22.2 109.1 %copy-start.3 = (bf16[1536,640]{0,1:T(8,128)(2,1)}, bf16[1536,640]{0,1:T(8,128)(2,1)S(1)}, u32[]{:S(2)}) copy-start(bf16[1536,640]{0,1:T(8,128)(2,1)S(1)} %copy.128) | copy-start | bytes 5898244
  22.7 26.0 %copy-start.63 = (f32[1536]{0:T(1024)}, f32[1536]{0:T(1024)S(1)}, u32[]{:S(2)}) copy-start(f32[1536]{0:T(1024)S(1)} %fusion.33) | copy-start | bytes 18436
  22.7 32.8 %copy-start.55 = (f32[1536]{0:T(1024)}, f32[1536]{0:T(1024)S(1)}, u32[]{:S(2)}) copy-start(f32[1536]{0:T(1024)S(1)} %fusion.115) | copy-start | bytes 18436
  22.7 55.9 %copy-start.61 = (f32[1536]{0:T(1024)}, f32[1536]{0:T(1024)S(1)}, u32[]{:S(2)}) copy-start(f32[1536]{0:T(1024)S(1)} %subtract_convert_fusion.1) | copy-start | bytes 18436
  47.8 7.7 %copy-start.66 = (f32[640]{0:T(1024)}, f32[640]{0:T(1024)S(1)}, u32[]{:S(2)}) copy-start(f32[640]{0:T(1024)S(1)} %get-tuple-element.109) | copy-start | bytes 7684
  59.8 50.7 %copy-start.18 = (bf16[1536,512]{0,1:T(8,128)(2,1)}, bf16[1536,512]{0,1:T(8,128)(2,1)S(1)}, u32[]{:S(2)}) copy-start(bf16[1536,512]{0,1:T(8,128)(2,1)S(1)} %get-tuple-element.151) | copy-start | bytes 4718596
  59.8 53.6 %collective-permute-start = (bf16[128,640]{1,0:T(8,128)(2,1)}, bf16[128,640]{1,0:T(8,128)(2,1)}, u32[]{:S(2)}, u32[]{:S(2)}) collective-permute-start(bf16[128,640]{1,0:T(8,128)(2,1)} %param.21), channel_id=1, source_target_pairs={{0,4},{4,8},{8,12},{12,16},{16,20},{20,24},{24,28},{28,0},{1,5},{5... | collective-permute-start | bytes 491528 | tf_op jit(solution)/shard_map/ppermute | solution.py:88
  60.0 56.6 %collective-permute-start.1 = (bf16[128,640]{1,0:T(8,128)(2,1)}, bf16[128,640]{1,0:T(8,128)(2,1)}, u32[]{:S(2)}, u32[]{:S(2)}) collective-permute-start(bf16[128,640]{1,0:T(8,128)(2,1)} %param.21), channel_id=1, source_target_pairs={{0,8},{4,12},{8,16},{12,20},{16,24},{20,28},{24,0},{28,4},{1,9},{5... | collective-permute-start | bytes 491528 | tf_op jit(solution)/shard_map/ppermute | solution.py:88
  61.5 57.5 %collective-permute-start.2 = (bf16[128,640]{1,0:T(8,128)(2,1)}, bf16[128,640]{1,0:T(8,128)(2,1)}, u32[]{:S(2)}, u32[]{:S(2)}) collective-permute-start(bf16[128,640]{1,0:T(8,128)(2,1)} %param.21), channel_id=1, source_target_pairs={{0,12},{4,16},{8,20},{12,24},{16,28},{20,0},{24,4},{28,8},{1,13},{... | collective-permute-start | bytes 491528 | tf_op jit(solution)/shard_map/ppermute | solution.py:88
  62.3 57.6 %collective-permute-start.3 = (bf16[128,640]{1,0:T(8,128)(2,1)}, bf16[128,640]{1,0:T(8,128)(2,1)}, u32[]{:S(2)}, u32[]{:S(2)}) collective-permute-start(bf16[128,640]{1,0:T(8,128)(2,1)} %param.21), channel_id=1, source_target_pairs={{0,16},{4,20},{8,24},{12,28},{16,0},{20,4},{24,8},{28,12},{1,17},{... | collective-permute-start | bytes 491528 | tf_op jit(solution)/shard_map/ppermute | solution.py:88
  65.1 55.8 %collective-permute-start.4 = (bf16[128,640]{1,0:T(8,128)(2,1)}, bf16[128,640]{1,0:T(8,128)(2,1)}, u32[]{:S(2)}, u32[]{:S(2)}) collective-permute-start(bf16[128,640]{1,0:T(8,128)(2,1)} %param.21), channel_id=1, source_target_pairs={{0,20},{4,24},{8,28},{12,0},{16,4},{20,8},{24,12},{28,16},{1,21},{... | collective-permute-start | bytes 491528 | tf_op jit(solution)/shard_map/ppermute | solution.py:88
  77.0 8.8 %copy-start.65 = (f32[1536]{0:T(1024)}, f32[1536]{0:T(1024)S(1)}, u32[]{:S(2)}) copy-start(f32[1536]{0:T(1024)S(1)} %multiply_reduce_fusion.14) | copy-start | bytes 18436
  92.4 16.3 %copy-start.23 = (bf16[1536,4,128]{2,0,1:T(8,128)(2,1)}, bf16[1536,4,128]{2,0,1:T(8,128)(2,1)S(1)}, u32[]{:S(2)}) copy-start(bf16[1536,4,128]{2,0,1:T(8,128)(2,1)S(1)} %get-tuple-element.132) | copy-start | bytes 4718596
  92.4 16.3 %copy-start.26 = (bf16[1536,4,128]{2,0,1:T(8,128)(2,1)}, bf16[1536,4,128]{2,0,1:T(8,128)(2,1)S(1)}, u32[]{:S(2)}) copy-start(bf16[1536,4,128]{2,0,1:T(8,128)(2,1)S(1)} %get-tuple-element.133) | copy-start | bytes 4718596
  112.1 19.1 %copy-start.31 = (bf16[1536,4,256]{0,2,1:T(8,128)(2,1)}, bf16[1536,4,256]{0,2,1:T(8,128)(2,1)S(1)}, u32[]{:S(2)}) copy-start(bf16[1536,4,256]{0,2,1:T(8,128)(2,1)S(1)} %pad_maximum_fusion.2) | copy-start | bytes 9437188
  113.4 14.8 %collective-permute-start.5 = (bf16[128,640]{1,0:T(8,128)(2,1)}, bf16[128,640]{1,0:T(8,128)(2,1)S(1)}, u32[]{:S(2)}, u32[]{:S(2)}) collective-permute-start(bf16[128,640]{1,0:T(8,128)(2,1)} %param.21), channel_id=1, source_target_pairs={{0,24},{4,28},{8,0},{12,4},{16,8},{20,12},{24,16},{28,20},{1,25},{... | collective-permute-start | bytes 491528 | tf_op jit(solution)/shard_map/ppermute | solution.py:88
  116.6 12.3 %collective-permute-start.6 = (bf16[128,640]{1,0:T(8,128)(2,1)}, bf16[128,640]{1,0:T(8,128)(2,1)S(1)}, u32[]{:S(2)}, u32[]{:S(2)}) collective-permute-start(bf16[128,640]{1,0:T(8,128)(2,1)} %param.21), channel_id=1, source_target_pairs={{0,28},{4,0},{8,4},{12,8},{16,12},{20,16},{24,20},{28,24},{1,29},{... | collective-permute-start | bytes 491528 | tf_op jit(solution)/shard_map/ppermute | solution.py:88
  135.6 10.5 %copy-start.35 = (bf16[1536,640]{0,1:T(8,128)(2,1)}, bf16[1536,640]{0,1:T(8,128)(2,1)S(1)}, u32[]{:S(2)}) copy-start(bf16[1536,640]{0,1:T(8,128)(2,1)S(1)} %multiply_convert_fusion.2) | copy-start | bytes 5898244
  175.6 7.5 %copy-start.12 = (bf16[1536,640]{0,1:T(8,128)(2,1)S(1)}, bf16[1536,640]{0,1:T(8,128)(2,1)}, u32[]{:S(2)}) copy-start(bf16[1536,640]{0,1:T(8,128)(2,1)} %copy.145) | copy-start | bytes 5898244
  175.6 7.5 %copy-start.71 = (f32[640]{0:T(1024)S(1)}, f32[640]{0:T(1024)}, u32[]{:S(2)}) copy-start(f32[640]{0:T(1024)} %get-tuple-element.106) | copy-start | bytes 7684
  175.6 7.5 %copy-start.80 = (pred[1536]{0:T(1024)(128)(4,1)S(1)}, pred[1536]{0:T(1024)(128)(4,1)}, u32[]{:S(2)}) copy-start(pred[1536]{0:T(1024)(128)(4,1)} %iota_compare_fusion.2) | copy-start | bytes 4612
  195.8 174.5 %reduce-scatter.8.cloned.1.call-start = ((), (), s32[]{:S(2)}) async-start(), calls=%async_computation.10 | async-start | bytes 2949120 | tf_op jit(solution)/shard_map/reduce_scatter | solution.py:61
  229.6 9.4 %copy-start.77 = (f32[4,512]{1,0:T(4,128)S(1)}, f32[4,512]{1,0:T(4,128)}, u32[]{:S(2)}) copy-start(f32[4,512]{1,0:T(4,128)} %copy-done.76) | copy-start | bytes 24580
  229.6 9.4 %copy-start.79 = (f32[4,512]{1,0:T(4,128)S(1)}, f32[4,512]{1,0:T(4,128)}, u32[]{:S(2)}) copy-start(f32[4,512]{1,0:T(4,128)} %copy-done.78) | copy-start | bytes 24580
  229.6 9.5 %copy-start.73 = (f32[4,512]{1,0:T(4,128)S(1)}, f32[4,512]{1,0:T(4,128)}, u32[]{:S(2)}) copy-start(f32[4,512]{1,0:T(4,128)} %copy-done.72) | copy-start | bytes 24580
  229.6 9.5 %copy-start.75 = (f32[4,512]{1,0:T(4,128)S(1)}, f32[4,512]{1,0:T(4,128)}, u32[]{:S(2)}) copy-start(f32[4,512]{1,0:T(4,128)} %copy-done.74) | copy-start | bytes 24580
  239.0 131.4 %reduce-scatter.10.cloned.1.call-start = ((), (), s32[]{:S(2)}) async-start(), calls=%async_computation.11 | async-start | bytes 2949120 | tf_op jit(solution)/shard_map/reduce_scatter | solution.py:61
  239.7 159.0 %reduce-scatter.12.cloned.1.call-start = ((), (), s32[]{:S(2)}) async-start(), calls=%async_computation.12 | async-start | bytes 1474560 | tf_op jit(solution)/shard_map/reduce_scatter | solution.py:61
  239.8 7.9 %copy-start.7 = (f32[1536,640]{0,1:T(8,128)S(1)}, f32[1536,640]{0,1:T(8,128)}, u32[]{:S(2)}) copy-start(f32[1536,640]{0,1:T(8,128)} %copy-done.5) | copy-start | bytes 11796484
  239.8 7.9 %copy-start.85 = (bf16[640,2048]{1,0:T(8,128)(2,1)S(1)}, bf16[640,2048]{1,0:T(8,128)(2,1)}, u32[]{:S(2)}) copy-start(bf16[640,2048]{1,0:T(8,128)(2,1)} %all-gather.9.cloned.1.call-done) | copy-start | bytes 7864324
  247.7 7.4 %copy-start.11 = (f32[1536,640]{0,1:T(8,128)S(1)}, f32[1536,640]{0,1:T(8,128)}, u32[]{:S(2)}) copy-start(f32[1536,640]{0,1:T(8,128)} %copy-done.10) | copy-start | bytes 11796484
  271.0 162.7 %reduce-scatter.14.cloned.1.call-start = ((), (), s32[]{:S(2)}) async-start(), calls=%async_computation.13 | async-start | bytes 2396160 | tf_op jit(solution)/shard_map/reduce_scatter | solution.py:61
  274.5 20.7 %copy-start.13 = (bf16[1536,4,256]{2,0,1:T(8,128)(2,1)}, bf16[1536,4,256]{2,0,1:T(8,128)(2,1)S(1)}, u32[]{:S(2)}) copy-start(bf16[1536,4,256]{2,0,1:T(8,128)(2,1)S(1)} %copy.148) | copy-start | bytes 9437188
  281.4 7.6 %copy-start.2 = (f32[4,512,512]{1,2,0:T(8,128)S(1)}, f32[4,512,512]{1,2,0:T(8,128)}, u32[]{:S(2)}) copy-start(f32[4,512,512]{1,2,0:T(8,128)} %copy-done.1) | copy-start | bytes 12582916
  281.4 13.8 %slice-start = ((s8[12582912]{0:T(1024)(128)(4,1)}), s8[4194304]{0:T(1024)(128)(4,1)S(1)}, s32[]{:S(2)}) async-start(s8[12582912]{0:T(1024)(128)(4,1)} %bitcast.161), calls=%async_computation.14 | async-start | bytes 8388608
  281.4 13.8 %slice-start.1 = ((s8[12582912]{0:T(1024)(128)(4,1)}), s8[4194304]{0:T(1024)(128)(4,1)S(1)}, s32[]{:S(2)}) async-start(s8[12582912]{0:T(1024)(128)(4,1)} %bitcast.161), calls=%async_computation.15 | async-start | bytes 8388608
  293.7 64.9 %collective-permute-start.7 = (bf16[256,640]{1,0:T(8,128)(2,1)}, bf16[256,640]{1,0:T(8,128)(2,1)}, u32[]{:S(2)}, u32[]{:S(2)}) collective-permute-start(bf16[256,640]{1,0:T(8,128)(2,1)} %reduce-scatter.6.cloned.1.call-done), channel_id=1, source_target_pairs={{0,1},{1,0},{2,3},{3,2},{4,5},{5,4},{6,7},{7,6},{8,9},{9,8},{10,11... | collective-permute-start | bytes 983048 | tf_op jit(solution)/shard_map/ppermute | solution.py:74
  301.4 13.1 %slice-start.7 = ((s8[8388608]{0:T(1024)(128)(4,1)}), s8[4194304]{0:T(1024)(128)(4,1)S(1)}, s32[]{:S(2)}) async-start(s8[8388608]{0:T(1024)(128)(4,1)} %bitcast.167), calls=%async_computation.21 | async-start | bytes 8388608
  301.4 7.9 %copy-start.39 = (bf16[1536,128]{0,1:T(8,128)(2,1)S(1)}, bf16[1536,128]{0,1:T(8,128)(2,1)}, u32[]{:S(2)}) copy-start(bf16[1536,128]{0,1:T(8,128)(2,1)} %get-tuple-element.142) | copy-start | bytes 1179652
  301.4 13.1 %slice-start.8 = ((s8[8388608]{0:T(1024)(128)(4,1)}), s8[4194304]{0:T(1024)(128)(4,1)S(1)}, s32[]{:S(2)}) async-start(s8[8388608]{0:T(1024)(128)(4,1)} %bitcast.167), calls=%async_computation.22 | async-start | bytes 8388608
  327.2 9.7 %slice-start.3 = ((s8[6291456]{0:T(1024)(128)(4,1)}), s8[4194304]{0:T(1024)(128)(4,1)S(1)}, s32[]{:S(2)}) async-start(s8[6291456]{0:T(1024)(128)(4,1)} %bitcast.163), calls=%async_computation.17 | async-start | bytes 8388608
  359.8 10.5 %copy-start.62 = (f32[1536]{0:T(1024)S(1)}, f32[1536]{0:T(1024)}, u32[]{:S(2)}) copy-start(f32[1536]{0:T(1024)} %copy-done.61) | copy-start | bytes 18436
  359.8 10.5 %copy-start.84 = (f32[128]{0:T(128)S(1)}, f32[128]{0:T(128)}, u32[]{:S(2)}) copy-start(f32[128]{0:T(128)} %negate_power_fusion) | copy-start | bytes 1540
  359.8 9.6 %collective-permute-start.8 = (bf16[256,640]{1,0:T(8,128)(2,1)S(1)}, bf16[256,640]{1,0:T(8,128)(2,1)S(1)}, u32[]{:S(2)}, u32[]{:S(2)}) collective-permute-start(bf16[256,640]{1,0:T(8,128)(2,1)S(1)} %add_convert_fusion.4), channel_id=1, source_target_pairs={{0,2},{1,3},{2,0},{3,1},{4,6},{5,7},{6,4},{7,5},{8,10},{9,11},{10,... | collective-permute-start | bytes 983048 | tf_op jit(solution)/shard_map/ppermute | solution.py:74
  373.4 9.7 %copy-start.4 = (bf16[1536,640]{0,1:T(8,128)(2,1)S(1)}, bf16[1536,640]{0,1:T(8,128)(2,1)}, u32[]{:S(2)}) copy-start(bf16[1536,640]{0,1:T(8,128)(2,1)} %copy-done.3) | copy-start | bytes 5898244
  373.5 9.7 %copy-start.56 = (f32[1536]{0:T(1024)S(1)}, f32[1536]{0:T(1024)}, u32[]{:S(2)}) copy-start(f32[1536]{0:T(1024)} %copy-done.55) | copy-start | bytes 18436
  402.8 7.8 %copy-start.64 = (f32[1536]{0:T(1024)S(1)}, f32[1536]{0:T(1024)}, u32[]{:S(2)}) copy-start(f32[1536]{0:T(1024)} %copy-done.63) | copy-start | bytes 18436
  402.9 8.8 %copy-start.9 = (f32[1536,640]{0,1:T(8,128)S(1)}, f32[1536,640]{0,1:T(8,128)}, u32[]{:S(2)}) copy-start(f32[1536,640]{0,1:T(8,128)} %copy-done.8) | copy-start | bytes 11796484
  402.9 7.8 %collective-permute-start.11 = (bf16[128,640]{1,0:T(8,128)(2,1)S(1)}, bf16[128,640]{1,0:T(8,128)(2,1)S(1)}, u32[]{:S(2)}, u32[]{:S(2)}) collective-permute-start(bf16[128,640]{1,0:T(8,128)(2,1)S(1)} %copy-done.57), channel_id=1, source_target_pairs={{0,2},{1,3},{2,0},{3,1},{4,6},{5,7},{6,4},{7,5},{8,10},{9,11},{10,... | collective-permute-start | bytes 491528 | tf_op jit(solution)/shard_map/ppermute | solution.py:74
  404.4 18.0 %collective-permute-start.13 = (bf16[80,2048]{1,0:T(8,128)(2,1)S(1)}, bf16[80,2048]{1,0:T(8,128)(2,1)S(1)}, u32[]{:S(2)}, u32[]{:S(2)}) collective-permute-start(bf16[80,2048]{1,0:T(8,128)(2,1)S(1)} %copy-done.52), channel_id=1, source_target_pairs={{0,2},{1,3},{2,0},{3,1},{4,6},{5,7},{6,4},{7,5},{8,10},{9,11},{10,... | collective-permute-start | bytes 983048 | tf_op jit(solution)/shard_map/ppermute | solution.py:74
  410.8 10.9 %collective-permute-start.12 = (bf16[128,640]{1,0:T(8,128)(2,1)S(1)}, bf16[128,640]{1,0:T(8,128)(2,1)S(1)}, u32[]{:S(2)}, u32[]{:S(2)}) collective-permute-start(bf16[128,640]{1,0:T(8,128)(2,1)S(1)} %add_convert_fusion.6), channel_id=1, source_target_pairs={{0,1},{1,0},{2,3},{3,2},{4,5},{5,4},{6,7},{7,6},{8,9},{9,8},{10,11... | collective-permute-start | bytes 491528 | tf_op jit(solution)/shard_map/ppermute | solution.py:74
  420.4 28.7 %copy-start.47 = (bf16[80,1024]{1,0:T(8,128)(2,1)S(1)}, bf16[80,1024]{1,0:T(8,128)(2,1)}, u32[]{:S(2)}) copy-start(bf16[80,1024]{1,0:T(8,128)(2,1)} %param.19) | copy-start | bytes 491524
  420.4 29.6 %copy-start.51 = (bf16[80,512]{1,0:T(8,128)(2,1)S(1)}, bf16[80,512]{1,0:T(8,128)(2,1)}, u32[]{:S(2)}) copy-start(bf16[80,512]{1,0:T(8,128)(2,1)} %param.20) | copy-start | bytes 245764
  420.4 10.7 %collective-permute-start.15 = (bf16[80,2048]{1,0:T(8,128)(2,1)S(1)}, bf16[80,2048]{1,0:T(8,128)(2,1)S(1)}, u32[]{:S(2)}, u32[]{:S(2)}) collective-permute-start(bf16[80,2048]{1,0:T(8,128)(2,1)S(1)} %copy-done.53), channel_id=1, source_target_pairs={{0,1},{1,0},{2,3},{3,2},{4,5},{5,4},{6,7},{7,6},{8,9},{9,8},{10,11... | collective-permute-start | bytes 983048 | tf_op jit(solution)/shard_map/ppermute | solution.py:74
  422.4 29.9 %copy-start.83 = (bf16[80]{0:T(256)(128)(2,1)S(1)}, bf16[80]{0:T(256)(128)(2,1)}, u32[]{:S(2)}) copy-start(bf16[80]{0:T(256)(128)(2,1)} %param.25) | copy-start | bytes 484
  422.5 15.3 %collective-permute-start.14 = (bf16[80,2048]{1,0:T(8,128)(2,1)S(1)}, bf16[80,2048]{1,0:T(8,128)(2,1)S(1)}, u32[]{:S(2)}, u32[]{:S(2)}) collective-permute-start(bf16[80,2048]{1,0:T(8,128)(2,1)S(1)} %add_convert_fusion.3), channel_id=1, source_target_pairs={{0,1},{1,0},{2,3},{3,2},{4,5},{5,4},{6,7},{7,6},{8,9},{9,8},{10,11... | collective-permute-start | bytes 983048 | tf_op jit(solution)/shard_map/ppermute | solution.py:74
  431.2 12.8 %collective-permute-start.16 = (bf16[80,2048]{1,0:T(8,128)(2,1)S(1)}, bf16[80,2048]{1,0:T(8,128)(2,1)S(1)}, u32[]{:S(2)}, u32[]{:S(2)}) collective-permute-start(bf16[80,2048]{1,0:T(8,128)(2,1)S(1)} %add_convert_fusion.2), channel_id=1, source_target_pairs={{0,2},{1,3},{2,0},{3,1},{4,6},{5,7},{6,4},{7,5},{8,10},{9,11},{10,... | collective-permute-start | bytes 983048 | tf_op jit(solution)/shard_map/ppermute | solution.py:74
  433.7 7.8 %collective-permute-start.9 = (bf16[80,1664]{1,0:T(8,128)(2,1)}, bf16[80,1664]{1,0:T(8,128)(2,1)S(1)}, u32[]{:S(2)}, u32[]{:S(2)}) collective-permute-start(bf16[80,1664]{1,0:T(8,128)(2,1)} %reduce-scatter.14.cloned.1.call-done), channel_id=1, source_target_pairs={{0,1},{1,0},{2,3},{3,2},{4,5},{5,4},{6,7},{7,6},{8,9},{9,8},{10,11... | collective-permute-start | bytes 798728 | tf_op jit(solution)/shard_map/ppermute | solution.py:74
  442.5 6.5 %collective-permute-start.10 = (bf16[80,1664]{1,0:T(8,128)(2,1)S(1)}, bf16[80,1664]{1,0:T(8,128)(2,1)S(1)}, u32[]{:S(2)}, u32[]{:S(2)}) collective-permute-start(bf16[80,1664]{1,0:T(8,128)(2,1)S(1)} %add_convert_fusion.5), channel_id=1, source_target_pairs={{0,2},{1,3},{2,0},{3,1},{4,6},{5,7},{6,4},{7,5},{8,10},{9,11},{10,... | collective-permute-start | bytes 798728 | tf_op jit(solution)/shard_map/ppermute | solution.py:74
  (60 other events, 232.6 us)
Sparse Core Ops, SparseCore 0:
  13.8 32.0 all-gather.4
  47.5 54.5 all-gather.6
  103.8 37.2 all-gather.8
  142.6 32.8 all-gather.10
  195.9 36.5 reduce-scatter.5
  239.1 36.3 reduce-scatter.7
  277.7 36.5 reduce-scatter.9
  316.7 32.1 reduce-scatter.11
  398.9 34.7 reduce-scatter.13
